TPU v7x, 32 devices: a whole 2x2x4 slice. The times are simulated.
32 devices in a mesh: gx: 4 (over x, core), gy: 4 (over z), gz: 2 (over y).
Axes of the slice: x: 2, y: 2, z: 4, core: 2. Of those that a mesh axis runs over, the one named last changes fastest.
Arguments:
- wave: float32 [64, 128, 256], P('gx', 'gy', 'gz'), may hold values from -7 to 7
- external: float32 [64, 128, 256], P('gx', 'gy', 'gz'), may hold values from 0 to 2
- weights: float32 [3, 17], replicated, may hold values from 0.02 to 0.1
Outputs:
- wave_next: float32 [64, 128, 256], P('gx', 'gy', 'gz')
- correlation: float32 [64, 128, 256], P('gx', 'gy', 'gz')
All inputs are finite; a program needn't handle non-finite values.
Results may differ from a plain program's by a relative error of at most 0.00029.
Values sent between devices are 32-bit elements; how exact they have to be, the bound alone decides.
A program may use at most 64 MiB of HBM per device.

v0:
```python
import jax
import jax.numpy as jnp
from jax import lax
from jax.sharding import PartitionSpec as P

SUBSTEPS = 3


LAP_COEF = (-205.0 / 72.0, 8.0 / 5.0, -1.0 / 5.0, 8.0 / 315.0, -1.0 / 560.0)
FORMS = ("jyz,ji->iyz", "xjz,ji->xiz", "xyj,ji->xyi")


def with_halo(cells, sides, width):
    for axis, dim in sides:
        count = lax.axis_size(axis)
        ends = count - 1
        head = lax.slice_in_dim(cells, 0, width, axis=dim)
        tail = lax.slice_in_dim(cells, cells.shape[dim] - width, cells.shape[dim], axis=dim)
        cells = jnp.concatenate(
            [
                lax.ppermute(tail, axis, [(i, (i + 1) % count) for i in range(ends)]),
                cells,
                lax.ppermute(head, axis, [((i + 1) % count, i) for i in range(ends)]),
            ],
            axis=dim,
        )
    return cells


def band_matrix(row, size_in, flip):
    size_out = size_in - 16
    rows_at = lax.broadcasted_iota(jnp.int32, (size_in, size_out), 0)
    cols_at = lax.broadcasted_iota(jnp.int32, (size_in, size_out), 1)
    offset = rows_at - cols_at
    if flip:
        offset = 16 - offset
    taps = jnp.arange(17, dtype=jnp.int32)
    return jnp.sum(jnp.where(offset[:, :, None] == taps, row, 0.0), axis=2)


def smear(padded, weights, flip):
    for dim in range(3):
        matrix = band_matrix(weights[dim], padded.shape[dim], flip)
        padded = jnp.einsum(FORMS[dim], padded, matrix, precision=lax.Precision.HIGHEST)
    return padded


def trim(field, margin):
    return field[margin:-margin, margin:-margin, margin:-margin]


def laplace(padded):
    center = trim(padded, 4)
    total = 3.0 * LAP_COEF[0] * center
    for dim in range(3):
        length = center.shape[dim]
        for step in range(1, 5):
            upper = [slice(4, -4), slice(4, -4), slice(4, -4)]
            lower = [slice(4, -4), slice(4, -4), slice(4, -4)]
            upper[dim] = slice(4 + step, 4 + step + length)
            lower[dim] = slice(4 - step, 4 - step + length)
            total = total + LAP_COEF[step] * (padded[tuple(upper)] + padded[tuple(lower)])
    return total


def inside_mask(shape, margin):
    index_list = (lax.axis_index("gx"), lax.axis_index("gy"), lax.axis_index("gz"))
    extent_list = (lax.axis_size("gx"), lax.axis_size("gy"), lax.axis_size("gz"))
    masks = []
    for dim in range(3):
        count = shape[dim]
        anchor = index_list[dim] * count - margin
        places = anchor + jnp.arange(count + 2 * margin, dtype=jnp.int32)
        masks.append(((places >= 0) & (places < count * extent_list[dim])).astype(jnp.float32))
    return masks[0][:, None, None] * masks[1][None, :, None] * masks[2][None, None, :]


def shards(wave, external, weights):
    density = wave * wave
    density_near = with_halo(density, (("gx", 0), ("gy", 1), ("gz", 2)), 8)
    coarse = smear(density_near, weights, False)
    source = -1.0 * density * coarse + 0.5 * density * coarse * coarse
    source_near = with_halo(source, (("gx", 0), ("gy", 1), ("gz", 2)), 8)
    correlation = (
        -0.5 * coarse * coarse
        + 0.5 / 3.0 * coarse * coarse * coarse
        + smear(source_near, weights, True)
    )
    potential = correlation + external
    stacked = with_halo(jnp.stack([wave, potential]), (("gx", 1), ("gy", 2), ("gz", 3)), 12)
    psi = stacked[0]
    field = stacked[1]
    margin = 12
    for step in range(SUBSTEPS):
        margin = margin - 4
        center = trim(psi, 4)
        field = trim(field, 4)
        updated = center - 0.08 * (-0.5 * laplace(psi) + field * center)
        if margin > 0:
            updated = updated * inside_mask(wave.shape, margin)
        psi = updated
    total = lax.psum(jnp.sum(psi * psi), ("gx", "gy", "gz"))
    count = float(psi.size * lax.axis_size("gx") * lax.axis_size("gy") * lax.axis_size("gz"))
    wave_next = psi * lax.rsqrt(total / count + 1e-06)
    return (wave_next, correlation)


def solution(mesh):
    placed = (P("gx", "gy", "gz"), P("gx", "gy", "gz"), P())
    return jax.shard_map(
        shards,
        mesh=mesh,
        in_specs=placed,
        out_specs=(P("gx", "gy", "gz"), P("gx", "gy", "gz")),
        check_vma=False,
    )
```

profile of v0, /device:TPU:0, one launch (start us, length us, event | category | flops | bytes accessed | tf_op | source)
XLA Modules:
  0.0 185.6 jit_solution(193307686533516000)
XLA Ops:
  0.6 1.1 copy_multiply_fusion
  1.8 2.4 %collective-permute-start = (f32[8,32,128]{2,0,1:T(8,128)S(1)}, f32[8,32,128]{2,0,1:T(8,128)S(1)}, u32[]{:S(2)}, u32[]{:S(2)}) collective-permute-start(f32[8,32,128]{2,0,1:T(8,128)S(1)} %get-tuple-element.28), channel_id=1, source_target_pairs={{0,8},{8,16},{16,24},{1,9},{9,17},{17,25},{2,10},{10,18},{18,26},{... | collective-permute-start | bytes 393224 | tf_op jit(solution)/shard_map/ppermute | solution.py:21
  4.2 1.3 collective-permute-start.1
  5.5 0.8 slice_bitcast_fusion.2
  6.6 2.9 %collective-permute-done.1 = f32[8,32,128]{2,0,1:T(8,128)S(1)} collective-permute-done((f32[8,32,128]{2,0,1:T(8,128)S(1)}, f32[8,32,128]{2,0,1:T(8,128)S(1)}, u32[]{:S(2)}, u32[]{:S(2)}) %collective-permute-start.1) | collective-permute-done | bytes 131104 | tf_op jit(solution)/shard_map/ppermute | solution.py:23
  9.5 3.5 %collective-permute-start.2 = (f32[32,8,128]{2,0,1:T(8,128)S(1)}, f32[32,8,128]{2,0,1:T(8,128)S(1)}, u32[]{:S(2)}, u32[]{:S(2)}) collective-permute-start(f32[32,8,128]{2,0,1:T(8,128)S(1)} %get-tuple-element.24), channel_id=1, source_target_pairs={{0,2},{2,4},{4,6},{1,3},{3,5},{5,7},{8,10},{10,12},{12,14},{9,11},... | collective-permute-start | bytes 393224 | tf_op jit(solution)/shard_map/ppermute | solution.py:21
  13.0 1.3 collective-permute-start.3
  14.5 1.0 collective-permute-done.2
  15.5 4.4 %collective-permute-done.3 = f32[32,8,128]{2,0,1:T(8,128)S(1)} collective-permute-done((f32[32,8,128]{2,0,1:T(8,128)S(1)}, f32[32,8,128]{2,0,1:T(8,128)S(1)}, u32[]{:S(2)}, u32[]{:S(2)}) %collective-permute-start.3) | collective-permute-done | bytes 131104 | tf_op jit(solution)/shard_map/ppermute | solution.py:23
  20.3 0.4 copy.23
  20.7 3.4 %collective-permute-start.4 = (f32[32,48,8]{1,2,0:T(8,128)S(1)}, f32[32,48,8]{1,2,0:T(8,128)S(1)}, u32[]{:S(2)}, u32[]{:S(2)}) collective-permute-start(f32[32,48,8]{1,2,0:T(8,128)S(1)} %copy.23), channel_id=1, source_target_pairs={{0,1},{2,3},{4,5},{6,7},{8,9},{10,11},{12,13},{14,15},{16,17},{18,... | collective-permute-start | bytes 147464 | tf_op jit(solution)/shard_map/ppermute | solution.py:21
  24.1 0.4 copy.24
  24.6 1.3 collective-permute-start.5
  26.0 0.9 collective-permute-done.4
  26.9 0.7 copy.25
  27.6 4.4 %collective-permute-done.5 = f32[32,48,8]{1,2,0:T(8,128)S(1)} collective-permute-done((f32[32,48,8]{1,2,0:T(8,128)S(1)}, f32[32,48,8]{1,2,0:T(8,128)S(1)}, u32[]{:S(2)}, u32[]{:S(2)}) %collective-permute-start.5) | collective-permute-done | bytes 49184 | tf_op jit(solution)/shard_map/ppermute | solution.py:23
  32.0 0.7 copy.26
  32.7 1.3 fusion.29
  34.0 1.0 convolution_bitcast_fusion.1
  35.1 0.6 fusion.118
  35.7 0.3 add_multiply_fusion
  36.0 2.6 %collective-permute-start.6 = (f32[8,32,128]{2,0,1:T(8,128)S(1)}, f32[8,32,128]{2,0,1:T(8,128)S(1)}, u32[]{:S(2)}, u32[]{:S(2)}) collective-permute-start(f32[8,32,128]{2,0,1:T(8,128)S(1)} %get-tuple-element.26), channel_id=1, source_target_pairs={{0,8},{8,16},{16,24},{1,9},{9,17},{17,25},{2,10},{10,18},{18,26},{... | collective-permute-start | bytes 393224 | tf_op jit(solution)/shard_map/ppermute | solution.py:21
  38.6 1.3 collective-permute-start.7
  39.9 3.6 %collective-permute-done.7 = f32[8,32,128]{2,0,1:T(8,128)S(1)} collective-permute-done((f32[8,32,128]{2,0,1:T(8,128)S(1)}, f32[8,32,128]{2,0,1:T(8,128)S(1)}, u32[]{:S(2)}, u32[]{:S(2)}) %collective-permute-start.7) | collective-permute-done | bytes 131104 | tf_op jit(solution)/shard_map/ppermute | solution.py:23
  43.6 3.5 %collective-permute-start.8 = (f32[32,8,128]{2,0,1:T(8,128)S(1)}, f32[32,8,128]{2,0,1:T(8,128)S(1)}, u32[]{:S(2)}, u32[]{:S(2)}) collective-permute-start(f32[32,8,128]{2,0,1:T(8,128)S(1)} %get-tuple-element.22), channel_id=1, source_target_pairs={{0,2},{2,4},{4,6},{1,3},{3,5},{5,7},{8,10},{10,12},{12,14},{9,11},... | collective-permute-start | bytes 393224 | tf_op jit(solution)/shard_map/ppermute | solution.py:21
  47.0 1.3 collective-permute-start.9
  48.3 1.2 collective-permute-done.8
  49.5 4.4 %collective-permute-done.9 = f32[32,8,128]{2,0,1:T(8,128)S(1)} collective-permute-done((f32[32,8,128]{2,0,1:T(8,128)S(1)}, f32[32,8,128]{2,0,1:T(8,128)S(1)}, u32[]{:S(2)}, u32[]{:S(2)}) %collective-permute-start.9) | collective-permute-done | bytes 131104 | tf_op jit(solution)/shard_map/ppermute | solution.py:23
  54.3 0.4 copy.30
  54.7 1.5 collective-permute-start.10
  56.2 0.4 copy.31
  56.7 1.5 collective-permute-start.11
  58.1 0.7 collective-permute-done.10
  58.9 0.7 copy.32
  59.6 4.4 %collective-permute-done.11 = f32[32,48,8]{1,2,0:T(8,128)S(1)} collective-permute-done((f32[32,48,8]{1,2,0:T(8,128)S(1)}, f32[32,48,8]{1,2,0:T(8,128)S(1)}, u32[]{:S(2)}, u32[]{:S(2)}) %collective-permute-start.11) | collective-permute-done | bytes 49184 | tf_op jit(solution)/shard_map/ppermute | solution.py:23
  64.0 0.7 copy.33
  64.7 1.3 fusion.43
  66.0 1.0 convolution_bitcast_fusion
  67.1 0.6 convolution_add_fusion
  67.8 2.7 %collective-permute-start.12 = (f32[2,12,32,128]{3,2,1,0:T(8,128)S(1)}, f32[2,12,32,128]{3,2,1,0:T(8,128)S(1)}, u32[]{:S(2)}, u32[]{:S(2)}) collective-permute-start(f32[2,12,32,128]{3,2,1,0:T(8,128)S(1)} %get-tuple-element.20), channel_id=1, source_target_pairs={{0,8},{8,16},{16,24},{1,9},{9,17},{17,25},{2,10},{10,18},{18,26},{... | collective-permute-start | bytes 1179656 | tf_op jit(solution)/shard_map/ppermute | solution.py:21
  70.5 1.3 collective-permute-start.13
  71.9 3.9 %collective-permute-done.13 = f32[2,12,32,128]{3,2,1,0:T(8,128)S(1)} collective-permute-done((f32[2,12,32,128]{3,2,1,0:T(8,128)S(1)}, f32[2,12,32,128]{3,2,1,0:T(8,128)S(1)}, u32[]{:S(2)}, u32[]{:S(2)}) %collective-permute-start.13) | collective-permute-done | bytes 393248 | tf_op jit(solution)/shard_map/ppermute | solution.py:23
  76.2 3.5 %collective-permute-start.14 = (f32[2,40,12,128]{3,1,2,0:T(8,128)S(1)}, f32[2,40,12,128]{3,1,2,0:T(8,128)S(1)}, u32[]{:S(2)}, u32[]{:S(2)}) collective-permute-start(f32[2,40,12,128]{3,1,2,0:T(8,128)S(1)} %copy.35), channel_id=1, source_target_pairs={{0,2},{2,4},{4,6},{1,3},{3,5},{5,7},{8,10},{10,12},{12,14},{9,11},... | collective-permute-start | bytes 1474568 | tf_op jit(solution)/shard_map/ppermute | solution.py:21
  79.8 1.3 collective-permute-start.15
  81.3 4.7 %collective-permute-done.14 = f32[2,40,12,128]{3,1,2,0:T(8,128)S(1)} collective-permute-done((f32[2,40,12,128]{3,1,2,0:T(8,128)S(1)}, f32[2,40,12,128]{3,1,2,0:T(8,128)S(1)}, u32[]{:S(2)}, u32[]{:S(2)}) %collective-permute-start.14) | collective-permute-done | bytes 491552 | tf_op jit(solution)/shard_map/ppermute | solution.py:21
  86.1 4.8 %collective-permute-done.15 = f32[2,40,12,128]{3,1,2,0:T(8,128)} collective-permute-done((f32[2,40,12,128]{3,1,2,0:T(8,128)S(1)}, f32[2,40,12,128]{3,1,2,0:T(8,128)}, u32[]{:S(2)}, u32[]{:S(2)}) %collective-permute-start.15) | collective-permute-done | bytes 491552 | tf_op jit(solution)/shard_map/ppermute | solution.py:23
  90.9 1.1 copy.38
  92.4 0.6 copy-done.1
  92.9 2.1 %fusion.127 = (f32[2,40,56,12]{3,2,1,0:T(8,128)}, f32[2,40,56,12]{3,2,1,0:T(8,128)S(1)}) fusion(f32[2,40,56,128]{3,2,1,0:T(8,128)S(1)} %pad_maximum_fusion.1), kind=kLoop, calls=%fused_computation.219 | loop fusion | bytes 860160 | tf_op jit(solution)/shard_map/slice | solution.py:18
  95.1 3.2 %copy.39 = f32[2,40,56,12]{2,1,3,0:T(8,128)} copy(f32[2,40,56,12]{3,2,1,0:T(8,128)} %get-tuple-element.12) | data formatting | bytes 430080 | tf_op jit(solution)/shard_map/slice | solution.py:18
  98.2 2.3 %collective-permute-start.16 = (f32[2,40,56,12]{2,1,3,0:T(8,128)}, f32[2,40,56,12]{2,1,3,0:T(8,128)}, u32[]{:S(2)}, u32[]{:S(2)}) collective-permute-start(f32[2,40,56,12]{2,1,3,0:T(8,128)} %copy.39), channel_id=1, source_target_pairs={{0,1},{2,3},{4,5},{6,7},{8,9},{10,11},{12,13},{14,15},{16,17},{18,... | collective-permute-start | bytes 645128 | tf_op jit(solution)/shard_map/ppermute | solution.py:21
  100.5 1.6 copy.40
  102.1 1.5 collective-permute-start.17
  103.7 4.0 %collective-permute-done.16 = f32[2,40,56,12]{2,1,3,0:T(8,128)} collective-permute-done((f32[2,40,56,12]{2,1,3,0:T(8,128)}, f32[2,40,56,12]{2,1,3,0:T(8,128)}, u32[]{:S(2)}, u32[]{:S(2)}) %collective-permute-start.16) | collective-permute-done | bytes 215072 | tf_op jit(solution)/shard_map/ppermute | solution.py:21
  107.7 1.7 copy.41
  109.4 5.3 %collective-permute-done.17 = f32[2,40,56,12]{2,1,3,0:T(8,128)} collective-permute-done((f32[2,40,56,12]{2,1,3,0:T(8,128)}, f32[2,40,56,12]{2,1,3,0:T(8,128)}, u32[]{:S(2)}, u32[]{:S(2)}) %collective-permute-start.17) | collective-permute-done | bytes 215072 | tf_op jit(solution)/shard_map/ppermute | solution.py:23
  114.7 3.1 %copy.42 = f32[2,40,56,12]{3,2,1,0:T(8,128)} copy(f32[2,40,56,12]{2,1,3,0:T(8,128)} %collective-permute-done.17) | data formatting | bytes 430080 | tf_op jit(solution)/shard_map/ppermute | solution.py:23
  117.8 6.0 %pad_maximum_fusion = f32[2,40,56,152]{3,2,1,0:T(8,128)S(1)} fusion(f32[2,40,56,12]{3,2,1,0:T(8,128)} %copy.42, f32[2,40,12,128]{3,2,1,0:T(8,128)} %copy-done.1, f32[2,12,32,128]{3,2,1,0:T(8,128)} %copy-done.3, f32[1,16,32,128]{3,2,1,0:T(8,128)S(1)} %add_bitcast_fusion, f32[1,16,32,128]{3,2,1,0:T(8,128)S(1)} %bitcast.40, f32[2,12,32,128]{3,2,1,0:T(8,128)} %copy-done.2, ...), kind=kLoop, calls=%fused_computation | loop fusion | flops 4766720 | bytes 5447680 | tf_op jit(solution)/shard_map/concatenate | solution.py:19
  123.8 0.3 slice_bitcast_fusion.1
  124.1 11.0 %fusion.3 = f32[32,48,144]{2,1,0:T(8,128)S(1)} fusion(f32[40,56,152]{2,1,0:T(8,128)S(1)} %get-tuple-element.11, f32[40,56,152]{2,1,0:T(8,128)S(1)} %get-tuple-element.10, f32[144]{0:T(256)S(1)} %and_convert_fusion.3, f32[32,48]{1,0:T(8,128)S(1)} %broadcast_multiply_fusion.1), kind=kLoop, calls=%fused_computation.8 | loop fusion | flops 9732096 | bytes 23894592 | tf_op jit(solution)/shard_map/mul | solution.py:100
  135.1 6.8 %fusion.60 = f32[24,40,136]{2,1,0:T(8,128)S(1)} fusion(f32[40,56,152]{2,1,0:T(8,128)S(1)} %get-tuple-element.11, f32[32,48,144]{2,1,0:T(8,128)S(1)} %fusion.3, f32[136]{0:T(256)S(1)} %and_convert_fusion, f32[24,40]{1,0:T(8,128)S(1)} %broadcast_multiply_fusion.2), kind=kLoop, calls=%fused_computation.86 | loop fusion | flops 5744640 | bytes 14104864 | tf_op jit(solution)/shard_map/mul | solution.py:100
  142.0 2.4 %multiply_reduce_fusion = (f32[]{:T(128)}, f32[16,32,128]{2,1,0:T(8,128)S(1)}) fusion(f32[40,56,152]{2,1,0:T(8,128)S(1)} %get-tuple-element.11, f32[24,40,136]{2,1,0:T(8,128)S(1)} %fusion.60), kind=kLoop, calls=%fused_computation.180 | loop fusion | flops 2883583 | bytes 7077892 | tf_op jit(solution)/shard_map/reduce_sum | solution.py:102
  144.3 39.8 %psum.7 = f32[]{:T(128)} all-reduce(f32[]{:T(128)} %get-tuple-element.8), channel_id=1, replica_groups=mesh['gx'=4,'gy'=4,'gz'=2] {'gx','gy','gz'}, use_global_device_ids=true, to_apply=%region_7.8 | all-reduce | flops 1 | bytes 8 | tf_op jit(solution)/shard_map/psum | solution.py:102
  184.9 0.7 broadcast_multiply_fusion
  (44 shorter events, 2.6 us)
Async XLA Ops:
  1.8 4.9 %collective-permute-start = (f32[8,32,128]{2,0,1:T(8,128)S(1)}, f32[8,32,128]{2,0,1:T(8,128)S(1)}, u32[]{:S(2)}, u32[]{:S(2)}) collective-permute-start(f32[8,32,128]{2,0,1:T(8,128)S(1)} %get-tuple-element.28), channel_id=1, source_target_pairs={{0,8},{8,16},{16,24},{1,9},{9,17},{17,25},{2,10},{10,18},{18,26},{... | collective-permute-start | bytes 393224 | tf_op jit(solution)/shard_map/ppermute | solution.py:21
  4.2 5.3 %collective-permute-start.1 = (f32[8,32,128]{2,0,1:T(8,128)S(1)}, f32[8,32,128]{2,0,1:T(8,128)S(1)}, u32[]{:S(2)}, u32[]{:S(2)}) collective-permute-start(f32[8,32,128]{2,0,1:T(8,128)S(1)} %get-tuple-element.29), channel_id=1, source_target_pairs={{8,0},{16,8},{24,16},{9,1},{17,9},{25,17},{10,2},{18,10},{26,18},{... | collective-permute-start | bytes 393224 | tf_op jit(solution)/shard_map/ppermute | solution.py:23
  9.5 6.0 %collective-permute-start.2 = (f32[32,8,128]{2,0,1:T(8,128)S(1)}, f32[32,8,128]{2,0,1:T(8,128)S(1)}, u32[]{:S(2)}, u32[]{:S(2)}) collective-permute-start(f32[32,8,128]{2,0,1:T(8,128)S(1)} %get-tuple-element.24), channel_id=1, source_target_pairs={{0,2},{2,4},{4,6},{1,3},{3,5},{5,7},{8,10},{10,12},{12,14},{9,11},... | collective-permute-start | bytes 393224 | tf_op jit(solution)/shard_map/ppermute | solution.py:21
  13.0 6.9 %collective-permute-start.3 = (f32[32,8,128]{2,0,1:T(8,128)S(1)}, f32[32,8,128]{2,0,1:T(8,128)S(1)}, u32[]{:S(2)}, u32[]{:S(2)}) collective-permute-start(f32[32,8,128]{2,0,1:T(8,128)S(1)} %get-tuple-element.25), channel_id=1, source_target_pairs={{2,0},{4,2},{6,4},{3,1},{5,3},{7,5},{10,8},{12,10},{14,12},{11,9},... | collective-permute-start | bytes 393224 | tf_op jit(solution)/shard_map/ppermute | solution.py:23
  20.7 6.2 %collective-permute-start.4 = (f32[32,48,8]{1,2,0:T(8,128)S(1)}, f32[32,48,8]{1,2,0:T(8,128)S(1)}, u32[]{:S(2)}, u32[]{:S(2)}) collective-permute-start(f32[32,48,8]{1,2,0:T(8,128)S(1)} %copy.23), channel_id=1, source_target_pairs={{0,1},{2,3},{4,5},{6,7},{8,9},{10,11},{12,13},{14,15},{16,17},{18,... | collective-permute-start | bytes 147464 | tf_op jit(solution)/shard_map/ppermute | solution.py:21
  24.6 7.4 %collective-permute-start.5 = (f32[32,48,8]{1,2,0:T(8,128)S(1)}, f32[32,48,8]{1,2,0:T(8,128)S(1)}, u32[]{:S(2)}, u32[]{:S(2)}) collective-permute-start(f32[32,48,8]{1,2,0:T(8,128)S(1)} %copy.24), channel_id=1, source_target_pairs={{1,0},{3,2},{5,4},{7,6},{9,8},{11,10},{13,12},{15,14},{17,16},{19,... | collective-permute-start | bytes 147464 | tf_op jit(solution)/shard_map/ppermute | solution.py:23
  34.0 1.6 copy-start
  36.0 3.9 %collective-permute-start.6 = (f32[8,32,128]{2,0,1:T(8,128)S(1)}, f32[8,32,128]{2,0,1:T(8,128)S(1)}, u32[]{:S(2)}, u32[]{:S(2)}) collective-permute-start(f32[8,32,128]{2,0,1:T(8,128)S(1)} %get-tuple-element.26), channel_id=1, source_target_pairs={{0,8},{8,16},{16,24},{1,9},{9,17},{17,25},{2,10},{10,18},{18,26},{... | collective-permute-start | bytes 393224 | tf_op jit(solution)/shard_map/ppermute | solution.py:21
  38.6 4.9 %collective-permute-start.7 = (f32[8,32,128]{2,0,1:T(8,128)S(1)}, f32[8,32,128]{2,0,1:T(8,128)S(1)}, u32[]{:S(2)}, u32[]{:S(2)}) collective-permute-start(f32[8,32,128]{2,0,1:T(8,128)S(1)} %get-tuple-element.27), channel_id=1, source_target_pairs={{8,0},{16,8},{24,16},{9,1},{17,9},{25,17},{10,2},{18,10},{26,18},{... | collective-permute-start | bytes 393224 | tf_op jit(solution)/shard_map/ppermute | solution.py:23
  43.6 6.0 %collective-permute-start.8 = (f32[32,8,128]{2,0,1:T(8,128)S(1)}, f32[32,8,128]{2,0,1:T(8,128)S(1)}, u32[]{:S(2)}, u32[]{:S(2)}) collective-permute-start(f32[32,8,128]{2,0,1:T(8,128)S(1)} %get-tuple-element.22), channel_id=1, source_target_pairs={{0,2},{2,4},{4,6},{1,3},{3,5},{5,7},{8,10},{10,12},{12,14},{9,11},... | collective-permute-start | bytes 393224 | tf_op jit(solution)/shard_map/ppermute | solution.py:21
  47.0 6.9 %collective-permute-start.9 = (f32[32,8,128]{2,0,1:T(8,128)S(1)}, f32[32,8,128]{2,0,1:T(8,128)S(1)}, u32[]{:S(2)}, u32[]{:S(2)}) collective-permute-start(f32[32,8,128]{2,0,1:T(8,128)S(1)} %get-tuple-element.23), channel_id=1, source_target_pairs={{2,0},{4,2},{6,4},{3,1},{5,3},{7,5},{10,8},{12,10},{14,12},{11,9},... | collective-permute-start | bytes 393224 | tf_op jit(solution)/shard_map/ppermute | solution.py:23
  54.7 4.1 %collective-permute-start.10 = (f32[32,48,8]{1,2,0:T(8,128)S(1)}, f32[32,48,8]{1,2,0:T(8,128)S(1)}, u32[]{:S(2)}, u32[]{:S(2)}) collective-permute-start(f32[32,48,8]{1,2,0:T(8,128)S(1)} %copy.30), channel_id=1, source_target_pairs={{0,1},{2,3},{4,5},{6,7},{8,9},{10,11},{12,13},{14,15},{16,17},{18,... | collective-permute-start | bytes 147464 | tf_op jit(solution)/shard_map/ppermute | solution.py:21
  56.7 7.3 %collective-permute-start.11 = (f32[32,48,8]{1,2,0:T(8,128)S(1)}, f32[32,48,8]{1,2,0:T(8,128)S(1)}, u32[]{:S(2)}, u32[]{:S(2)}) collective-permute-start(f32[32,48,8]{1,2,0:T(8,128)S(1)} %copy.31), channel_id=1, source_target_pairs={{1,0},{3,2},{5,4},{7,6},{9,8},{11,10},{13,12},{15,14},{17,16},{19,... | collective-permute-start | bytes 147464 | tf_op jit(solution)/shard_map/ppermute | solution.py:23
  66.0 1.6 copy-start.5
  67.6 8.2 %copy-start.4 = (f32[16,32,128]{2,1,0:T(8,128)}, f32[16,32,128]{2,1,0:T(8,128)S(1)}, u32[]{:S(2)}) copy-start(f32[16,32,128]{2,1,0:T(8,128)S(1)} %convolution_add_fusion) | copy-start | bytes 786436
  67.8 4.1 %collective-permute-start.12 = (f32[2,12,32,128]{3,2,1,0:T(8,128)S(1)}, f32[2,12,32,128]{3,2,1,0:T(8,128)S(1)}, u32[]{:S(2)}, u32[]{:S(2)}) collective-permute-start(f32[2,12,32,128]{3,2,1,0:T(8,128)S(1)} %get-tuple-element.20), channel_id=1, source_target_pairs={{0,8},{8,16},{16,24},{1,9},{9,17},{17,25},{2,10},{10,18},{18,26},{... | collective-permute-start | bytes 1179656 | tf_op jit(solution)/shard_map/ppermute | solution.py:21
  70.5 5.3 %collective-permute-start.13 = (f32[2,12,32,128]{3,2,1,0:T(8,128)S(1)}, f32[2,12,32,128]{3,2,1,0:T(8,128)S(1)}, u32[]{:S(2)}, u32[]{:S(2)}) collective-permute-start(f32[2,12,32,128]{3,2,1,0:T(8,128)S(1)} %get-tuple-element.21), channel_id=1, source_target_pairs={{8,0},{16,8},{24,16},{9,1},{17,9},{25,17},{10,2},{18,10},{26,18},{... | collective-permute-start | bytes 1179656 | tf_op jit(solution)/shard_map/ppermute | solution.py:23
  71.9 20.2 %copy-start.2 = (f32[2,12,32,128]{3,2,1,0:T(8,128)}, f32[2,12,32,128]{3,2,1,0:T(8,128)S(1)}, u32[]{:S(2)}) copy-start(f32[2,12,32,128]{3,2,1,0:T(8,128)S(1)} %collective-permute-done.12) | copy-start | bytes 1179652
  75.8 16.3 %copy-start.3 = (f32[2,12,32,128]{3,2,1,0:T(8,128)}, f32[2,12,32,128]{3,2,1,0:T(8,128)S(1)}, u32[]{:S(2)}) copy-start(f32[2,12,32,128]{3,2,1,0:T(8,128)S(1)} %collective-permute-done.13) | copy-start | bytes 1179652
  76.2 9.8 %collective-permute-start.14 = (f32[2,40,12,128]{3,1,2,0:T(8,128)S(1)}, f32[2,40,12,128]{3,1,2,0:T(8,128)S(1)}, u32[]{:S(2)}, u32[]{:S(2)}) collective-permute-start(f32[2,40,12,128]{3,1,2,0:T(8,128)S(1)} %copy.35), channel_id=1, source_target_pairs={{0,2},{2,4},{4,6},{1,3},{3,5},{5,7},{8,10},{10,12},{12,14},{9,11},... | collective-permute-start | bytes 1474568 | tf_op jit(solution)/shard_map/ppermute | solution.py:21
  79.8 11.1 %collective-permute-start.15 = (f32[2,40,12,128]{3,1,2,0:T(8,128)S(1)}, f32[2,40,12,128]{3,1,2,0:T(8,128)}, u32[]{:S(2)}, u32[]{:S(2)}) collective-permute-start(f32[2,40,12,128]{3,1,2,0:T(8,128)S(1)} %copy.36), channel_id=1, source_target_pairs={{2,0},{4,2},{6,4},{3,1},{5,3},{7,5},{10,8},{12,10},{14,12},{11,9},... | collective-permute-start | bytes 1474568 | tf_op jit(solution)/shard_map/ppermute | solution.py:23
  92.1 0.9 copy-start.1
  98.2 9.4 %collective-permute-start.16 = (f32[2,40,56,12]{2,1,3,0:T(8,128)}, f32[2,40,56,12]{2,1,3,0:T(8,128)}, u32[]{:S(2)}, u32[]{:S(2)}) collective-permute-start(f32[2,40,56,12]{2,1,3,0:T(8,128)} %copy.39), channel_id=1, source_target_pairs={{0,1},{2,3},{4,5},{6,7},{8,9},{10,11},{12,13},{14,15},{16,17},{18,... | collective-permute-start | bytes 645128 | tf_op jit(solution)/shard_map/ppermute | solution.py:21
  102.1 12.6 %collective-permute-start.17 = (f32[2,40,56,12]{2,1,3,0:T(8,128)}, f32[2,40,56,12]{2,1,3,0:T(8,128)}, u32[]{:S(2)}, u32[]{:S(2)}) collective-permute-start(f32[2,40,56,12]{2,1,3,0:T(8,128)} %copy.40), channel_id=1, source_target_pairs={{1,0},{3,2},{5,4},{7,6},{9,8},{11,10},{13,12},{15,14},{17,16},{19,... | collective-permute-start | bytes 645128 | tf_op jit(solution)/shard_map/ppermute | solution.py:23
where the time goes:
time: 187 us; the launch traced here: 186 us
  waiting for transfers between devices  50.6 us (27%)
  blocking collectives  39.8 us (21%)
  starting transfers between devices  37.4 us (20%)
  other arithmetic  29.7 us (16%)
  local copies, waits for them, and re-layouts  20.3 us (11%)
  matrix products  5.86 us (3%)
  between operations  1.9 us (1%)
    psum x1, blocking collectives, shards(): total = lax.psum(jnp.sum(psi * psi), ('gx', 'gy', 'gz'))  39.8 us
    ppermute x9, waiting for transfers between devices, with_halo(): lax.ppermute(head, axis, [((i + 1) % count, i) for i in range(ends)])  38 us
    ppermute x9, starting transfers between devices, with_halo(): lax.ppermute(tail, axis, [(i, (i + 1) % count) for i in range(ends)])  25.4 us
    mul x2, other arithmetic, shards(): updated = updated * inside_mask(wave.shape, margin)  17.8 us
    ppermute x9, waiting for transfers between devices, with_halo(): lax.ppermute(tail, axis, [(i, (i + 1) % count) for i in range(ends)])  12.6 us
    ppermute x9, starting transfers between devices, with_halo(): lax.ppermute(head, axis, [((i + 1) % count, i) for i in range(ends)])  12 us
    slice x10, local copies, waits for them, and re-layouts, with_halo(): lax.slice_in_dim(cells, cells.shape[dim] - width, cells.shape[dim], axis=...  7.06 us
    concatenate x5, other arithmetic, with_halo(): jnp.concatenate([lax.ppermute(tail, axis, [(i, (i + 1) % count) for i in...  6.51 us
  transfers between devices with their start and end apart: 18, of which 15 were waited for; matrix products, arithmetic and copies ran while one was open for 4% of the time, Pallas kernels for 0%

commit v1 on v0

v1 whole, which is shorter than its diff:
```python
import functools

import jax
import jax.numpy as jnp
from jax import lax
from jax.experimental import pallas as pl
from jax.experimental.pallas import tpu as pltpu
from jax.sharding import PartitionSpec as P

SUBSTEPS = 3
LAP_COEF = (-205.0 / 72.0, 8.0 / 5.0, -1.0 / 5.0, 8.0 / 315.0, -1.0 / 560.0)
STEP = 0.08
AXES = ("gx", "gy", "gz")
MESH = pl.DeviceIdType.MESH
R = 8
H = 4


def lanes(shape):
    return lax.broadcasted_iota(jnp.int32, shape, len(shape) - 1)


def lane_taps(mid, low, high, step, taps):
    at = lanes(mid.shape)
    width = mid.shape[-1]
    total = None
    for k, tap in taps:
        if k == 0:
            part = mid
        elif k > 0:
            s = k * step
            part = pltpu.roll(jnp.where(at < s, high, mid), width - s, mid.ndim - 1)
        else:
            s = -k * step
            part = pltpu.roll(jnp.where(at >= width - s, low, mid), s, mid.ndim - 1)
        part = part * tap
        total = part if total is None else total + part
    return total


def kernel(sizes, w_ref, wave_ref, ext_ref, out_ref, corr_ref,
           wb, sb, xc, yb, pyb, psi, va, pack, zin, sums, sums2,
           send, recv, send2, recv2):
    nx, ny, nz = sizes
    cx, cy, cz = wave_ref.shape
    ix, iy, iz = (lax.axis_index(a) for a in AXES)
    plane = nx * nz
    per = cz // cx
    here = ix * nz + iz

    def plane_id(d):
        t = lax.rem(here + d, plane)
        return t, {"gx": lax.div(t, nz), "gz": lax.rem(t, nz)}

    def line_id(d):
        t = lax.rem(iy + d, ny)
        return t, {"gy": t}

    barrier = pltpu.get_barrier_semaphore()

    def greet(ids):
        def body(d, c):
            pl.semaphore_signal(barrier, inc=1, device_id=ids(d)[1], device_id_type=MESH)
            return c
        return body

    lax.fori_loop(1, plane, greet(plane_id), 0)
    lax.fori_loop(1, ny, greet(line_id), 0)

    counter = [0]

    def message(src, dst, dx, dy, dz):
        k = counter[0]
        counter[0] += 1
        to, back = None, None
        for d, i, n in ((dx, ix, nx), (dy, iy, ny), (dz, iz, nz)):
            if d > 0:
                a, b = i < n - 1, i > 0
            elif d < 0:
                a, b = i > 0, i < n - 1
            else:
                continue
            to = a if to is None else to & a
            back = b if back is None else back & b
        target = {}
        for name, d, i, n in zip(AXES, (dx, dy, dz), (ix, iy, iz), sizes):
            if d:
                target[name] = jnp.clip(i + d, 0, n - 1)
        copy = pltpu.make_async_remote_copy(
            src_ref=src, dst_ref=dst, send_sem=send.at[k], recv_sem=recv.at[k],
            device_id=target, device_id_type=MESH)
        return copy, to, back, dst

    sent = []

    def start(messages):
        for copy, to, _, _ in messages:
            pl.when(to)(copy.start)
            sent.append((copy, to))

    def blank(messages):
        for _, _, back, dst in messages:
            @pl.when(jnp.logical_not(back))
            def _(dst=dst):
                dst[...] = jnp.zeros(dst.shape, dst.dtype)

    def arrive(messages):
        for copy, _, back, _ in messages:
            pl.when(back)(copy.wait_recv)

    at = lanes((cy, cz))
    zero = jnp.zeros((cy, cz), jnp.float32)

    def pack_one(i, value, packs):
        mine = (at >= per * i) & (at < per * i + per)
        low = pltpu.roll(value, per * i, 1)
        high = pltpu.roll(value, lax.rem(per * i + per, cz), 1)
        return jnp.where(mine, low, packs[0]), jnp.where(mine, high, packs[1])

    def unpack(i, from_low, from_high):
        a = pltpu.roll(from_high, lax.rem(cz - per * i, cz), 1)
        b = pltpu.roll(from_low, cz - per - per * i, 1)
        return jnp.where(at < per, a, b)

    def pack_out(slot, packs):
        pack[slot, 0] = packs[0]
        pack[slot, 1] = packs[1]

    def z_messages(slot, across):
        out = []
        for dx in ((-1, 0, 1) if across else (0,)):
            out.append(message(pack.at[slot, 1], zin.at[slot, 0, 1 - dx], dx, 0, 1))
            out.append(message(pack.at[slot, 0], zin.at[slot, 1, 1 - dx], dx, 0, -1))
        return out

    def stage(i, packs):
        value = wave_ref[i]
        wb[R + i, pl.ds(R, cy)] = value
        return pack_one(i, value, packs)

    pack_out(0, lax.fori_loop(0, cx, stage, (zero, zero)))

    wave_x = [
        message(wave_ref.at[pl.ds(cx - R, R)], wb.at[pl.ds(0, R), pl.ds(R, cy)], 1, 0, 0),
        message(wave_ref.at[pl.ds(0, R)], wb.at[pl.ds(R + cx, R), pl.ds(R, cy)], -1, 0, 0),
    ]
    wave_z = z_messages(0, True)
    wave_y = [
        message(wave_ref.at[:, pl.ds(cy - R, R)], wb.at[pl.ds(R, cx), pl.ds(0, R)], 0, 1, 0),
        message(wave_ref.at[:, pl.ds(0, R)], wb.at[pl.ds(R, cx), pl.ds(R + cy, R)], 0, -1, 0),
    ]

    def y_messages(buf):
        return [
            message(buf.at[:, pl.ds(cy, R)], buf.at[:, pl.ds(0, R)], 0, 1, 0),
            message(buf.at[:, pl.ds(R, R)], buf.at[:, pl.ds(R + cy, R)], 0, -1, 0),
        ]

    mid_y = y_messages(yb.at[0])
    src_x = [
        message(sb.at[pl.ds(cx, R)], sb.at[pl.ds(0, R)], 1, 0, 0),
        message(sb.at[pl.ds(R, R)], sb.at[pl.ds(R + cx, R)], -1, 0, 0),
    ]
    src_z = z_messages(1, True)
    end_y = y_messages(yb.at[1])

    psi_moves = []
    for s in range(SUBSTEPS - 1):
        buf = psi.at[s]
        moves = [
            message(buf.at[pl.ds(cx, H), pl.ds(R, cy)], buf.at[pl.ds(0, H), pl.ds(R, cy)], 1, 0, 0),
            message(buf.at[pl.ds(H, H), pl.ds(R, cy)], buf.at[pl.ds(H + cx, H), pl.ds(R, cy)], -1, 0, 0),
        ]
        own = pl.ds(H, cx)
        moves += [
            message(buf.at[own, pl.ds(cy, R)], buf.at[own, pl.ds(0, R)], 0, 1, 0),
            message(buf.at[own, pl.ds(R, R)], buf.at[own, pl.ds(R + cy, R)], 0, -1, 0),
        ]
        moves += z_messages(2 + s, False)
        psi_moves.append(moves)

    pl.semaphore_wait(barrier, plane - 1 + ny - 1)
    start(wave_x + wave_z + wave_y)
    for group in [wave_x, wave_z, wave_y, mid_y, src_x, src_z, end_y] + psi_moves:
        blank(group)

    def taps_of(dim, flip):
        return [(k, w_ref[dim, R - k if flip else R + k]) for k in range(-R, R + 1)]

    def smear_xz(src, y_at, slot, square, flip, buf):
        taps = taps_of(0, flip)

        def x_pass(j, c):
            rows = pl.ds(pl.multiple_of(y_at + 8 * j, 8), 8)
            ins = [src[k, rows] for k in range(cx + 2 * R)]
            if square:
                ins = [v * v for v in ins]
            for i in range(cx):
                total = None
                for k, tap in taps:
                    part = ins[i + R + k] * tap
                    total = part if total is None else total + part
                xc[i, pl.ds(pl.multiple_of(8 * j, 8), 8)] = total
            return c

        lax.fori_loop(0, cy // 8, x_pass, 0)
        sides = []
        for side in range(2):
            near = [zin[slot, side, place] for place in range(3)]
            if square:
                near = [v * v for v in near]
            sides.append(near)
        below = lane_taps(sides[0][1], sides[0][0], sides[0][2], per, taps)
        above = lane_taps(sides[1][1], sides[1][0], sides[1][2], per, taps)
        taps_z = taps_of(2, flip)

        def z_pass(i, c):
            near = unpack(i, below, above)
            buf[i, pl.ds(R, cy)] = lane_taps(xc[i], near, near, 1, taps_z)
            return c

        lax.fori_loop(0, cx, z_pass, 0)

    def smear_y(buf, i, taps):
        total = None
        for k, tap in taps:
            part = buf[i, pl.ds(R + k, cy)] * tap
            total = part if total is None else total + part
        return total

    arrive(wave_x + wave_z)
    smear_xz(wb, R, 0, True, False, yb.at[0])
    start(mid_y)
    arrive(mid_y)
    taps_y = taps_of(1, False)

    def source_pass(i, packs):
        coarse = smear_y(yb.at[0], i, taps_y)
        value = wave_ref[i]
        dens = value * value
        both = coarse * coarse
        source = 0.5 * dens * both - dens * coarse
        corr_ref[i] = (0.5 / 3.0) * both * coarse - 0.5 * both
        sb[R + i] = source
        return pack_one(i, source, packs)

    pack_out(1, lax.fori_loop(0, cx, source_pass, (zero, zero)))

    start(src_x + src_z)
    arrive(src_x + src_z)
    smear_xz(sb, 0, 1, False, True, yb.at[1])
    start(end_y)
    arrive(end_y)
    taps_yt = taps_of(1, True)

    def corr_pass(i, c):
        corr = corr_ref[i] + smear_y(yb.at[1], i, taps_yt)
        corr_ref[i] = corr
        va[i] = (1.0 + STEP * 0.5 * 3.0 * LAP_COEF[0]) - STEP * (corr + ext_ref[i])
        return c

    lax.fori_loop(0, cx, corr_pass, 0)

    gains = [STEP * 0.5 * c for c in LAP_COEF]

    def advance(buf, reach, i, below, above):
        center = buf[reach + i, pl.ds(R, cy)]
        near = unpack(i, below, above)
        total = center * va[i]
        for k in range(1, H + 1):
            pair = buf[reach + i + k, pl.ds(R, cy)] + buf[reach + i - k, pl.ds(R, cy)]
            pair += buf[reach + i, pl.ds(R + k, cy)] + buf[reach + i, pl.ds(R - k, cy)]
            pair += pltpu.roll(jnp.where(at < k, near, center), cz - k, 1)
            pair += pltpu.roll(jnp.where(at >= cz - k, near, center), k, 1)
            total += gains[k] * pair
        return total

    arrive(wave_y)
    buf, reach, slot = wb, R, 0
    for s in range(SUBSTEPS):
        if s:
            arrive(psi_moves[s - 1])
        below, above = zin[slot, 0, 1], zin[slot, 1, 1]
        if s < SUBSTEPS - 1:
            after = psi.at[s]

            def middle(i, packs, buf=buf, reach=reach, below=below, above=above, after=after):
                value = advance(buf, reach, i, below, above)
                after[H + i, pl.ds(R, cy)] = value
                return pack_one(i, value, packs)

            pack_out(2 + s, lax.fori_loop(0, cx, middle, (zero, zero)))
            start(psi_moves[s])
            buf, reach, slot = after, H, 2 + s
        else:
            def last(i, total):
                value = advance(buf, reach, i, below, above)
                out_ref[i] = value
                return total + value * value

            total = lax.fori_loop(0, cx, last, zero)

    part = total[0:8]
    for j in range(1, cy // 8):
        part = part + total[8 * j:8 * j + 8]

    def all_sum(part, slots, ssem, rsem, me, n, ids):
        if n == 1:
            return part
        slots[n] = part

        def copy_of(d, slot):
            return pltpu.make_async_remote_copy(
                src_ref=slots.at[n], dst_ref=slots.at[slot], send_sem=ssem.at[d], recv_sem=rsem.at[slot],
                device_id=ids(d)[1], device_id_type=MESH)

        def go(d, c):
            copy_of(d, me).start()
            return c

        def come(d, c):
            t = ids(d)[0]
            copy_of(d, t).wait_recv()
            return c + slots[t]

        def left(d, c):
            copy_of(d, me).wait_send()
            return c

        lax.fori_loop(1, n, go, 0)
        total = lax.fori_loop(1, n, come, part)
        lax.fori_loop(1, n, left, 0)
        return total

    part = all_sum(part, sums, send2.at[0], recv2.at[0], here, plane, plane_id)
    part = all_sum(part, sums2, send2.at[1], recv2.at[1], iy, ny, line_id)
    cells = float(cx * cy * cz * nx * ny * nz)
    scale = lax.rsqrt(jnp.full((1, cz), jnp.sum(part), jnp.float32) / cells + 1e-06)

    def finish(i, c):
        out_ref[i] = out_ref[i] * scale
        return c

    lax.fori_loop(0, cx, finish, 0)
    for copy, to in sent:
        pl.when(to)(copy.wait_send)


def shards(sizes, wave, external, weights):
    cx, cy, cz = wave.shape
    nx, ny, nz = sizes
    f32 = jnp.float32
    n_messages = 36
    most = max(nx * nz, ny)
    vmem = pl.BlockSpec(memory_space=pltpu.VMEM)
    return pl.pallas_call(
        functools.partial(kernel, sizes),
        out_shape=(jax.ShapeDtypeStruct(wave.shape, f32), jax.ShapeDtypeStruct(wave.shape, f32)),
        in_specs=[pl.BlockSpec(memory_space=pltpu.SMEM), vmem, vmem],
        out_specs=(vmem, vmem),
        scratch_shapes=[
            pltpu.VMEM((cx + 2 * R, cy + 2 * R, cz), f32),
            pltpu.VMEM((cx + 2 * R, cy, cz), f32),
            pltpu.VMEM((cx, cy, cz), f32),
            pltpu.VMEM((2, cx, cy + 2 * R, cz), f32),
            pltpu.VMEM((8, cz), f32),
            pltpu.VMEM((SUBSTEPS - 1, cx + 2 * H, cy + 2 * R, cz), f32),
            pltpu.VMEM((cx, cy, cz), f32),
            pltpu.VMEM((SUBSTEPS + 1, 2, cy, cz), f32),
            pltpu.VMEM((SUBSTEPS + 1, 2, 3, cy, cz), f32),
            pltpu.VMEM((nx * nz + 1, 8, cz), f32),
            pltpu.VMEM((ny + 1, 8, cz), f32),
            pltpu.SemaphoreType.DMA((n_messages,)),
            pltpu.SemaphoreType.DMA((n_messages,)),
            pltpu.SemaphoreType.DMA((2, most)),
            pltpu.SemaphoreType.DMA((2, most)),
        ],
        compiler_params=pltpu.CompilerParams(collective_id=0, has_side_effects=True,
                                             vmem_limit_bytes=32 * 1024 * 1024),
    )(weights, wave, external)


def solution(mesh):
    sizes = tuple(mesh.shape[a] for a in AXES)
    spec = P(*AXES)
    return jax.shard_map(
        functools.partial(shards, sizes),
        mesh=mesh,
        in_specs=(spec, spec, P()),
        out_specs=(spec, spec),
        check_vma=False,
    )
```

time: 187 us -> 60.6 us (0.32)
  Pallas kernels: 0 us -> 55.7 us
  waiting for transfers between devices: 50.6 us -> 0 us
  blocking collectives: 39.8 us -> 0 us
  starting transfers between devices: 37.4 us -> 0 us
  other arithmetic: 29.7 us -> 0 us
  local copies, waits for them, and re-layouts: 20.3 us -> 3.98 us
  matrix products: 5.86 us -> 0 us
    pallas_call x0 -> x1, Pallas kernels: none -> 55.7 us  [shards(): pl.pallas_call(functools.partial(kernel, sizes), out_shape=(jax.ShapeDtyp...]
    ppermute x18 -> x0, waiting for transfers between devices: 50.6 us -> none  [the longest x9 38 us: with_halo(): lax.ppermute(head, axis, [((i + 1) % count, i) for i in range(ends)])]
    psum x1 -> x0, blocking collectives: 39.8 us -> none  [shards(): total = lax.psum(jnp.sum(psi * psi), ('gx', 'gy', 'gz'))]
    ppermute x18 -> x0, starting transfers between devices: 37.4 us -> none  [the longest x9 25.4 us: with_halo(): lax.ppermute(tail, axis, [(i, (i + 1) % count) for i in range(ends)])]
    mul x6 -> x0, other arithmetic: 19.8 us -> none  [the longest x2 17.8 us: shards(): updated = updated * inside_mask(wave.shape, margin)]
    slice x14 -> x0, local copies, waits for them, and re-layouts: 9.65 us -> none  [the longest x10 7.06 us: with_halo(): lax.slice_in_dim(cells, cells.shape[dim] - width, cells.shape[dim], axis=...]
    ppermute x8 -> x0, local copies, waits for them, and re-layouts: 8.89 us -> none  [the longest x4 5.65 us: with_halo(): lax.ppermute(head, axis, [((i + 1) % count, i) for i in range(ends)])]
    concatenate x5 -> x0, other arithmetic: 6.51 us -> none  [with_halo(): jnp.concatenate([lax.ppermute(tail, axis, [(i, (i + 1) % count) for i in...]
  transfers between devices with their start and end apart: 18 -> 0, of which waited for: 15 -> 0; matrix products, arithmetic and copies ran while one was open for 4% -> 0% of each run, Pallas kernels for 0% -> 0%
where the time goes in v1:
time: 60.6 us; the launch traced here: 60.4 us
  Pallas kernels  55.7 us (92%)
  local copies, waits for them, and re-layouts  3.98 us (7%)
  between operations  0.65 us (1%)
    pallas_call x1, Pallas kernels, shards(): pl.pallas_call(functools.partial(kernel, sizes), out_shape=(jax.ShapeDtyp...  55.7 us
    unnamed x8, local copies, waits for them, and re-layouts  3.98 us

profile of v1, /device:TPU:0, one launch (start us, length us, event | category | flops | bytes accessed | tf_op | source)
XLA Modules:
  0.0 60.4 jit_solution(12249719293599528611)
XLA Ops:
  0.6 0.0 copy-start
  0.6 0.9 %copy-done = f32[16,32,128]{2,1,0:T(8,128)S(1)} copy-done((f32[16,32,128]{2,1,0:T(8,128)S(1)}, f32[16,32,128]{2,1,0:T(8,128)}, u32[]{:S(2)}) %copy-start) | copy-done | bytes 262168
  1.6 0.0 copy-start.1
  1.6 0.9 %copy-done.1 = f32[16,32,128]{2,1,0:T(8,128)S(1)} copy-done((f32[16,32,128]{2,1,0:T(8,128)S(1)}, f32[16,32,128]{2,1,0:T(8,128)}, u32[]{:S(2)}) %copy-start.1) | copy-done | bytes 262168
  2.5 0.0 copy-start.2
  2.5 0.7 %copy-done.2 = f32[3,17]{1,0:T(4,128)S(1)} copy-done((f32[3,17]{1,0:T(4,128)S(1)}, f32[3,17]{1,0:T(4,128)}, u32[]{:S(2)}) %copy-start.2) | copy-done | bytes 228
  3.2 55.7 %shard_map.50 = (f32[16,32,128]{2,1,0:T(8,128)S(1)}, f32[16,32,128]{2,1,0:T(8,128)S(1)}) custom-call(f32[3,17]{1,0:T(4,128)S(1)} %copy-done.2, f32[16,32,128]{2,1,0:T(8,128)S(1)} %copy-done, f32[16,32,128]{2,1,0:T(8,128)S(1)} %copy-done.1), custom_call_target="tpu_custom_call" | custom-call | tf_op jit(solution)/shard_map/pallas_call | solution.py:356
  59.0 0.7 %copy.7 = f32[16,32,128]{2,1,0:T(8,128)} copy(f32[16,32,128]{2,1,0:T(8,128)S(1)} %get-tuple-element.4) | data formatting | bytes 524288
  59.7 0.7 %copy.8 = f32[16,32,128]{2,1,0:T(8,128)} copy(f32[16,32,128]{2,1,0:T(8,128)S(1)} %get-tuple-element.5) | data formatting | bytes 524288
Async XLA Ops:
  0.6 1.0 %copy-start = (f32[16,32,128]{2,1,0:T(8,128)S(1)}, f32[16,32,128]{2,1,0:T(8,128)}, u32[]{:S(2)}) copy-start(f32[16,32,128]{2,1,0:T(8,128)} %wave_ref.1) | copy-start | bytes 786436
  1.6 0.9 %copy-start.1 = (f32[16,32,128]{2,1,0:T(8,128)S(1)}, f32[16,32,128]{2,1,0:T(8,128)}, u32[]{:S(2)}) copy-start(f32[16,32,128]{2,1,0:T(8,128)} %ext_ref.1) | copy-start | bytes 786436
  2.5 0.7 %copy-start.2 = (f32[3,17]{1,0:T(4,128)S(1)}, f32[3,17]{1,0:T(4,128)}, u32[]{:S(2)}) copy-start(f32[3,17]{1,0:T(4,128)} %w_ref.1) | copy-start | bytes 616

commit v2 on v1

--- a/solution.py
+++ b/solution.py
@@ -36,6 +36,34 @@
         part = part * tap
         total = part if total is None else total + part
     return total
+
+
+UNROLL = {"stage": 16, "z": 4, "source": 4, "corr": 4, "sub": 4, "x": 1}
+
+
+def loop(name, n, body, init):
+    width = min(UNROLL[name], n)
+    if n % width:
+        width = 1
+    if width == n:
+        for i in range(n):
+            init = body(i, init)
+        return init
+
+    def step(j, carry):
+        for k in range(width):
+            carry = body(j * width + k, carry)
+        return carry
+
+    return lax.fori_loop(0, n // width, step, init)
+
+
+def turn(value, shift):
+    return value if isinstance(shift, int) and shift == 0 else pltpu.roll(value, shift, 1)
+
+
+def modulo(a, n):
+    return a % n if isinstance(a, int) else lax.rem(a, n)
 
 
 def kernel(sizes, w_ref, wave_ref, ext_ref, out_ref, corr_ref,
@@ -113,13 +141,13 @@
 
     def pack_one(i, value, packs):
         mine = (at >= per * i) & (at < per * i + per)
-        low = pltpu.roll(value, per * i, 1)
-        high = pltpu.roll(value, lax.rem(per * i + per, cz), 1)
+        low = turn(value, per * i)
+        high = turn(value, modulo(per * i + per, cz))
         return jnp.where(mine, low, packs[0]), jnp.where(mine, high, packs[1])
 
     def unpack(i, from_low, from_high):
-        a = pltpu.roll(from_high, lax.rem(cz - per * i, cz), 1)
-        b = pltpu.roll(from_low, cz - per - per * i, 1)
+        a = turn(from_high, modulo(cz - per * i, cz))
+        b = turn(from_low, cz - per - per * i)
         return jnp.where(at < per, a, b)
 
     def pack_out(slot, packs):
@@ -138,7 +166,7 @@
         wb[R + i, pl.ds(R, cy)] = value
         return pack_one(i, value, packs)
 
-    pack_out(0, lax.fori_loop(0, cx, stage, (zero, zero)))
+    pack_out(0, loop("stage", cx, stage, (zero, zero)))
 
     wave_x = [
         message(wave_ref.at[pl.ds(cx - R, R)], wb.at[pl.ds(0, R), pl.ds(R, cy)], 1, 0, 0),
@@ -203,7 +231,7 @@
                 xc[i, pl.ds(pl.multiple_of(8 * j, 8), 8)] = total
             return c
 
-        lax.fori_loop(0, cy // 8, x_pass, 0)
+        loop("x", cy // 8, x_pass, 0)
         sides = []
         for side in range(2):
             near = [zin[slot, side, place] for place in range(3)]
@@ -219,7 +247,7 @@
             buf[i, pl.ds(R, cy)] = lane_taps(xc[i], near, near, 1, taps_z)
             return c
 
-        lax.fori_loop(0, cx, z_pass, 0)
+        loop("z", cx, z_pass, 0)
 
     def smear_y(buf, i, taps):
         total = None
@@ -244,7 +272,7 @@
         sb[R + i] = source
         return pack_one(i, source, packs)
 
-    pack_out(1, lax.fori_loop(0, cx, source_pass, (zero, zero)))
+    pack_out(1, loop("source", cx, source_pass, (zero, zero)))
 
     start(src_x + src_z)
     arrive(src_x + src_z)
@@ -259,7 +287,7 @@
         va[i] = (1.0 + STEP * 0.5 * 3.0 * LAP_COEF[0]) - STEP * (corr + ext_ref[i])
         return c
 
-    lax.fori_loop(0, cx, corr_pass, 0)
+    loop("corr", cx, corr_pass, 0)
 
     gains = [STEP * 0.5 * c for c in LAP_COEF]
 
@@ -289,7 +317,7 @@
                 after[H + i, pl.ds(R, cy)] = value
                 return pack_one(i, value, packs)
 
-            pack_out(2 + s, lax.fori_loop(0, cx, middle, (zero, zero)))
+            pack_out(2 + s, loop("sub", cx, middle, (zero, zero)))
             start(psi_moves[s])
             buf, reach, slot = after, H, 2 + s
         else:
@@ -298,7 +326,7 @@
                 out_ref[i] = value
                 return total + value * value
 
-            total = lax.fori_loop(0, cx, last, zero)
+            total = loop("sub", cx, last, zero)
 
     part = total[0:8]
     for j in range(1, cy // 8):
@@ -341,7 +369,7 @@
         out_ref[i] = out_ref[i] * scale
         return c
 
-    lax.fori_loop(0, cx, finish, 0)
+    loop("corr", cx, finish, 0)
     for copy, to in sent:
         pl.when(to)(copy.wait_send)
 

time: 60.6 us -> 51.6 us (0.85)
  Pallas kernels: 55.7 us -> 46.8 us
    pallas_call x1, Pallas kernels: 55.7 us -> 46.8 us  [shards(): pl.pallas_call(functools.partial(kernel, sizes), out_shape=(jax.ShapeDtyp...]
where the time goes in v2:
time: 51.6 us; the launch traced here: 51.4 us
  Pallas kernels  46.8 us (91%)
  local copies, waits for them, and re-layouts  3.98 us (8%)
  between operations  0.65 us (1%)
    pallas_call x1, Pallas kernels, shards(): pl.pallas_call(functools.partial(kernel, sizes), out_shape=(jax.ShapeDtyp...  46.8 us
    unnamed x8, local copies, waits for them, and re-layouts  3.98 us

profile of v2, /device:TPU:0, one launch (start us, length us, event | category | flops | bytes accessed | tf_op | source)
XLA Modules:
  0.0 51.4 jit_solution(14471393230363568463)
XLA Ops:
  0.6 0.0 copy-start
  0.6 0.9 %copy-done = f32[16,32,128]{2,1,0:T(8,128)S(1)} copy-done((f32[16,32,128]{2,1,0:T(8,128)S(1)}, f32[16,32,128]{2,1,0:T(8,128)}, u32[]{:S(2)}) %copy-start) | copy-done | bytes 262168
  1.6 0.0 copy-start.1
  1.6 0.9 %copy-done.1 = f32[16,32,128]{2,1,0:T(8,128)S(1)} copy-done((f32[16,32,128]{2,1,0:T(8,128)S(1)}, f32[16,32,128]{2,1,0:T(8,128)}, u32[]{:S(2)}) %copy-start.1) | copy-done | bytes 262168
  2.5 0.0 copy-start.2
  2.5 0.7 %copy-done.2 = f32[3,17]{1,0:T(4,128)S(1)} copy-done((f32[3,17]{1,0:T(4,128)S(1)}, f32[3,17]{1,0:T(4,128)}, u32[]{:S(2)}) %copy-start.2) | copy-done | bytes 228
  3.2 46.8 %shard_map.50 = (f32[16,32,128]{2,1,0:T(8,128)S(1)}, f32[16,32,128]{2,1,0:T(8,128)S(1)}) custom-call(f32[3,17]{1,0:T(4,128)S(1)} %copy-done.2, f32[16,32,128]{2,1,0:T(8,128)S(1)} %copy-done, f32[16,32,128]{2,1,0:T(8,128)S(1)} %copy-done.1), custom_call_target="tpu_custom_call" | custom-call | tf_op jit(solution)/shard_map/pallas_call | solution.py:384
  50.0 0.7 %copy.7 = f32[16,32,128]{2,1,0:T(8,128)} copy(f32[16,32,128]{2,1,0:T(8,128)S(1)} %get-tuple-element.4) | data formatting | bytes 524288
  50.7 0.7 %copy.8 = f32[16,32,128]{2,1,0:T(8,128)} copy(f32[16,32,128]{2,1,0:T(8,128)S(1)} %get-tuple-element.5) | data formatting | bytes 524288
Async XLA Ops:
  0.6 1.0 %copy-start = (f32[16,32,128]{2,1,0:T(8,128)S(1)}, f32[16,32,128]{2,1,0:T(8,128)}, u32[]{:S(2)}) copy-start(f32[16,32,128]{2,1,0:T(8,128)} %wave_ref.1) | copy-start | bytes 786436
  1.6 0.9 %copy-start.1 = (f32[16,32,128]{2,1,0:T(8,128)S(1)}, f32[16,32,128]{2,1,0:T(8,128)}, u32[]{:S(2)}) copy-start(f32[16,32,128]{2,1,0:T(8,128)} %ext_ref.1) | copy-start | bytes 786436
  2.5 0.7 %copy-start.2 = (f32[3,17]{1,0:T(4,128)S(1)}, f32[3,17]{1,0:T(4,128)}, u32[]{:S(2)}) copy-start(f32[3,17]{1,0:T(4,128)} %w_ref.1) | copy-start | bytes 616

commit v3 on v2

--- a/solution.py
+++ b/solution.py
@@ -38,7 +38,8 @@
     return total
 
 
-UNROLL = {"stage": 16, "z": 4, "source": 4, "corr": 4, "sub": 4, "x": 1}
+UNROLL = {"stage": 16, "z": 2, "source": 4, "corr": 4, "sub": 4, "x": 1}
+ZW = 4
 
 
 def loop(name, n, body, init):
@@ -66,11 +67,17 @@
     return a % n if isinstance(a, int) else lax.rem(a, n)
 
 
-def kernel(sizes, w_ref, wave_ref, ext_ref, out_ref, corr_ref,
-           wb, sb, xc, yb, pyb, psi, va, pack, zin, sums, sums2,
-           send, recv, send2, recv2):
+def kernel(sizes, w_hbm, wave_hbm, ext_hbm, out_ref, corr_ref, scale_ref,
+           wb, sb, xc, yb, psi, va, pack, zin, ypack, yin, bands, ext_ref, w_ref, sums, sums2,
+           send, recv, send2, recv2, local):
     nx, ny, nz = sizes
-    cx, cy, cz = wave_ref.shape
+    cx, cy, cz = wave_hbm.shape
+    wave_ref = wb.at[pl.ds(R, cx), pl.ds(R, cy)]
+    get_wave = pltpu.make_async_copy(wave_hbm, wave_ref, local.at[0])
+    get_ext = pltpu.make_async_copy(ext_hbm, ext_ref, local.at[1])
+    get_weights = pltpu.make_async_copy(w_hbm, w_ref, local.at[2])
+    get_wave.start()
+    get_weights.start()
     ix, iy, iz = (lax.axis_index(a) for a in AXES)
     plane = nx * nz
     per = cz // cx
@@ -162,9 +169,9 @@
         return out
 
     def stage(i, packs):
-        value = wave_ref[i]
-        wb[R + i, pl.ds(R, cy)] = value
-        return pack_one(i, value, packs)
+        return pack_one(i, wave_ref[i], packs)
+
+    get_wave.wait()
 
     pack_out(0, loop("stage", cx, stage, (zero, zero)))
 
@@ -199,21 +206,43 @@
             message(buf.at[pl.ds(cx, H), pl.ds(R, cy)], buf.at[pl.ds(0, H), pl.ds(R, cy)], 1, 0, 0),
             message(buf.at[pl.ds(H, H), pl.ds(R, cy)], buf.at[pl.ds(H + cx, H), pl.ds(R, cy)], -1, 0, 0),
         ]
-        own = pl.ds(H, cx)
         moves += [
-            message(buf.at[own, pl.ds(cy, R)], buf.at[own, pl.ds(0, R)], 0, 1, 0),
-            message(buf.at[own, pl.ds(R, R)], buf.at[own, pl.ds(R + cy, R)], 0, -1, 0),
+            message(ypack.at[s, 1], yin.at[s, 0], 0, 1, 0),
+            message(ypack.at[s, 0], yin.at[s, 1], 0, -1, 0),
         ]
         moves += z_messages(2 + s, False)
         psi_moves.append(moves)
 
     pl.semaphore_wait(barrier, plane - 1 + ny - 1)
     start(wave_x + wave_z + wave_y)
+    get_ext.start()
+    get_weights.wait()
     for group in [wave_x, wave_z, wave_y, mid_y, src_x, src_z, end_y] + psi_moves:
         blank(group)
 
     def taps_of(dim, flip):
         return [(k, w_ref[dim, R - k if flip else R + k]) for k in range(-R, R + 1)]
+
+    row = lax.broadcasted_iota(jnp.int32, (cz, cz), 0)
+    gap = row - lanes((cz, cz))
+
+    def band(slot, taps):
+        inner = jnp.zeros((cz, cz), jnp.float32)
+        outer = inner
+        for k, tap in taps:
+            inner = jnp.where(gap == k, tap, inner)
+            if k:
+                outer = jnp.where(gap == (k - cz if k > 0 else k + cz), tap, outer)
+        bands[slot, pl.ds(0, cz)] = inner
+        bands[slot, pl.ds(cz, cz)] = outer
+
+    def along_z(values, nears, slot):
+        both = jnp.concatenate([jnp.concatenate(values, 0), jnp.concatenate(nears, 0)], 1)
+        return jnp.dot(both, bands[slot], precision=lax.Precision.HIGHEST,
+                       preferred_element_type=jnp.float32)
+
+    band(0, taps_of(2, False))
+    band(1, taps_of(2, True))
 
     def smear_xz(src, y_at, slot, square, flip, buf):
         taps = taps_of(0, flip)
@@ -240,14 +269,15 @@
             sides.append(near)
         below = lane_taps(sides[0][1], sides[0][0], sides[0][2], per, taps)
         above = lane_taps(sides[1][1], sides[1][0], sides[1][2], per, taps)
-        taps_z = taps_of(2, flip)
-
-        def z_pass(i, c):
-            near = unpack(i, below, above)
-            buf[i, pl.ds(R, cy)] = lane_taps(xc[i], near, near, 1, taps_z)
+
+        def z_pass(group, c):
+            these = [group * ZW + k for k in range(ZW)]
+            made = along_z([xc[i] for i in these], [unpack(i, below, above) for i in these], int(flip))
+            for k, i in enumerate(these):
+                buf[i, pl.ds(R, cy)] = made[k * cy:(k + 1) * cy]
             return c
 
-        loop("z", cx, z_pass, 0)
+        loop("z", cx // ZW, z_pass, 0)
 
     def smear_y(buf, i, taps):
         total = None
@@ -280,6 +310,8 @@
     start(end_y)
     arrive(end_y)
     taps_yt = taps_of(1, True)
+
+    get_ext.wait()
 
     def corr_pass(i, c):
         corr = corr_ref[i] + smear_y(yb.at[1], i, taps_yt)
@@ -308,6 +340,10 @@
     for s in range(SUBSTEPS):
         if s:
             arrive(psi_moves[s - 1])
+            for i in range(cx):
+                half = pl.ds(H * (i % 2), H)
+                buf[H + i, pl.ds(R - H, H)] = yin[s - 1, 0, i // 2, half]
+                buf[H + i, pl.ds(R + cy, H)] = yin[s - 1, 1, i // 2, half]
         below, above = zin[slot, 0, 1], zin[slot, 1, 1]
         if s < SUBSTEPS - 1:
             after = psi.at[s]
@@ -318,6 +354,10 @@
                 return pack_one(i, value, packs)
 
             pack_out(2 + s, loop("sub", cx, middle, (zero, zero)))
+            for i in range(cx):
+                half = pl.ds(H * (i % 2), H)
+                ypack[s, 0, i // 2, half] = after[H + i, pl.ds(R, H)]
+                ypack[s, 1, i // 2, half] = after[H + i, pl.ds(R + cy - H, H)]
             start(psi_moves[s])
             buf, reach, slot = after, H, 2 + s
         else:
@@ -363,13 +403,7 @@
     part = all_sum(part, sums, send2.at[0], recv2.at[0], here, plane, plane_id)
     part = all_sum(part, sums2, send2.at[1], recv2.at[1], iy, ny, line_id)
     cells = float(cx * cy * cz * nx * ny * nz)
-    scale = lax.rsqrt(jnp.full((1, cz), jnp.sum(part), jnp.float32) / cells + 1e-06)
-
-    def finish(i, c):
-        out_ref[i] = out_ref[i] * scale
-        return c
-
-    loop("corr", cx, finish, 0)
+    scale_ref[...] = lax.rsqrt(jnp.full(scale_ref.shape, jnp.sum(part), jnp.float32) / cells + 1e-06)
     for copy, to in sent:
         pl.when(to)(copy.wait_send)
 
@@ -381,31 +415,39 @@
     n_messages = 36
     most = max(nx * nz, ny)
     vmem = pl.BlockSpec(memory_space=pltpu.VMEM)
-    return pl.pallas_call(
+    stay = pl.BlockSpec(memory_space=pltpu.HBM)
+    psi, corr, scale = pl.pallas_call(
         functools.partial(kernel, sizes),
-        out_shape=(jax.ShapeDtypeStruct(wave.shape, f32), jax.ShapeDtypeStruct(wave.shape, f32)),
-        in_specs=[pl.BlockSpec(memory_space=pltpu.SMEM), vmem, vmem],
-        out_specs=(vmem, vmem),
+        out_shape=(jax.ShapeDtypeStruct(wave.shape, f32), jax.ShapeDtypeStruct(wave.shape, f32),
+                   jax.ShapeDtypeStruct((8, cz), f32)),
+        in_specs=[stay, stay, stay],
+        out_specs=(vmem, vmem, vmem),
         scratch_shapes=[
             pltpu.VMEM((cx + 2 * R, cy + 2 * R, cz), f32),
             pltpu.VMEM((cx + 2 * R, cy, cz), f32),
             pltpu.VMEM((cx, cy, cz), f32),
             pltpu.VMEM((2, cx, cy + 2 * R, cz), f32),
-            pltpu.VMEM((8, cz), f32),
             pltpu.VMEM((SUBSTEPS - 1, cx + 2 * H, cy + 2 * R, cz), f32),
             pltpu.VMEM((cx, cy, cz), f32),
             pltpu.VMEM((SUBSTEPS + 1, 2, cy, cz), f32),
             pltpu.VMEM((SUBSTEPS + 1, 2, 3, cy, cz), f32),
+            pltpu.VMEM((SUBSTEPS - 1, 2, cx // 2, 2 * H, cz), f32),
+            pltpu.VMEM((SUBSTEPS - 1, 2, cx // 2, 2 * H, cz), f32),
+            pltpu.VMEM((2, 2 * cz, cz), f32),
+            pltpu.VMEM((cx, cy, cz), f32),
+            pltpu.SMEM(weights.shape, f32),
             pltpu.VMEM((nx * nz + 1, 8, cz), f32),
             pltpu.VMEM((ny + 1, 8, cz), f32),
             pltpu.SemaphoreType.DMA((n_messages,)),
             pltpu.SemaphoreType.DMA((n_messages,)),
             pltpu.SemaphoreType.DMA((2, most)),
             pltpu.SemaphoreType.DMA((2, most)),
+            pltpu.SemaphoreType.DMA((3,)),
         ],
         compiler_params=pltpu.CompilerParams(collective_id=0, has_side_effects=True,
-                                             vmem_limit_bytes=32 * 1024 * 1024),
+                                             vmem_limit_bytes=67043328),
     )(weights, wave, external)
+    return psi * scale[0, 0], corr
 
 
 def solution(mesh):

time: 51.6 us -> 48.2 us (0.934)
  Pallas kernels: 46.8 us -> 43.1 us
  other arithmetic: 0 us -> 2.36 us
  local copies, waits for them, and re-layouts: 3.98 us -> 1.9 us
    pallas_call x1, Pallas kernels: 46.8 us -> 43.1 us  [shards(): pl.pallas_call(functools.partial(kernel, sizes), out_shape=(jax.ShapeDtyp...]
    unnamed x8 -> x3, local copies, waits for them, and re-layouts: 3.98 us -> 0.71 us
    mul x0 -> x1, other arithmetic: none -> 2.36 us  [shards(): return (psi * scale[0, 0], corr)]
    slice x0 -> x1, local copies, waits for them, and re-layouts: none -> 1.19 us  [shards(): return (psi * scale[0, 0], corr)]
where the time goes in v3:
time: 48.2 us; the launch traced here: 48 us
  Pallas kernels  43.1 us (89%)
  other arithmetic  2.36 us (5%)
  local copies, waits for them, and re-layouts  1.9 us (4%)
  between operations  0.64 us (1%)
    pallas_call x1, Pallas kernels, shards(): pl.pallas_call(functools.partial(kernel, sizes), out_shape=(jax.ShapeDtyp...  43.1 us
    mul x1, other arithmetic, shards(): return (psi * scale[0, 0], corr)  2.36 us
    slice x1, local copies, waits for them, and re-layouts, shards(): return (psi * scale[0, 0], corr)  1.19 us

profile of v3, /device:TPU:0, one launch (start us, length us, event | category | flops | bytes accessed | tf_op | source)
XLA Modules:
  0.0 48.0 jit_solution(9453325069199701974)
XLA Ops:
  0.6 43.1 %shard_map.50 = (f32[16,32,128]{2,1,0:T(8,128)}, f32[16,32,128]{2,1,0:T(8,128)}, f32[8,128]{1,0:T(8,128)}) custom-call(f32[3,17]{1,0:T(4,128)} %w_hbm.1, f32[16,32,128]{2,1,0:T(8,128)} %wave_hbm.1, f32[16,32,128]{2,1,0:T(8,128)} %ext_hbm.1), custom_call_target="tpu_custom_call" | custom-call | tf_op jit(solution)/shard_map/pallas_call | solution.py:419
  43.7 1.2 %slice.3 = f32[1,1]{1,0:T(1,128)} slice(f32[8,128]{1,0:T(8,128)} %get-tuple-element.6), slice={[0:1], [0:1]} | slice | bytes 8 | tf_op jit(solution)/shard_map/slice | solution.py:450
  44.9 0.0 copy-start
  44.9 2.4 %broadcast_multiply_fusion = f32[16,32,128]{2,1,0:T(8,128)} fusion(f32[16,32,128]{2,1,0:T(8,128)} %get-tuple-element.5, f32[]{:T(128)} %bitcast), kind=kLoop, calls=%fused_computation | loop fusion | flops 65536 | bytes 524292 | tf_op jit(solution)/shard_map/mul | solution.py:450
  47.3 0.0 copy-done
  47.3 0.7 %copy.6 = f32[16,32,128]{2,1,0:T(8,128)} copy(f32[16,32,128]{2,1,0:T(8,128)S(1)} %copy-done) | data formatting | bytes 524288
Async XLA Ops:
  44.9 2.4 %copy-start = (f32[16,32,128]{2,1,0:T(8,128)S(1)}, f32[16,32,128]{2,1,0:T(8,128)}, u32[]{:S(2)}) copy-start(f32[16,32,128]{2,1,0:T(8,128)} %get-tuple-element.11) | copy-start | bytes 786436

commit v4 on v3

--- a/solution.py
+++ b/solution.py
@@ -38,6 +38,7 @@
     return total
 
 
+PARTNERS = [(dx, 0, dz) for dx in (-1, 0, 1) for dz in (-1, 0, 1) if dx or dz] + [(0, 1, 0), (0, -1, 0)]
 UNROLL = {"stage": 16, "z": 2, "source": 4, "corr": 4, "sub": 4, "x": 1}
 ZW = 4
 
@@ -99,8 +100,26 @@
             return c
         return body
 
-    lax.fori_loop(1, plane, greet(plane_id), 0)
-    lax.fori_loop(1, ny, greet(line_id), 0)
+    near = nx <= 4 and ny <= 4 and nz <= 2
+    if near:
+        guests = 0
+        for dx, dy, dz in PARTNERS:
+            there = None
+            target = {}
+            for name, d, i, n in zip(AXES, (dx, dy, dz), (ix, iy, iz), sizes):
+                if d:
+                    ok = i < n - 1 if d > 0 else i > 0
+                    there = ok if there is None else there & ok
+                    target[name] = jnp.clip(i + d, 0, n - 1)
+            guests += there.astype(jnp.int32)
+
+            @pl.when(there)
+            def _(target=target):
+                pl.semaphore_signal(barrier, inc=1, device_id=target, device_id_type=MESH)
+    else:
+        guests = plane - 1 + ny - 1
+        lax.fori_loop(1, plane, greet(plane_id), 0)
+        lax.fori_loop(1, ny, greet(line_id), 0)
 
     counter = [0]
 
@@ -213,7 +232,7 @@
         moves += z_messages(2 + s, False)
         psi_moves.append(moves)
 
-    pl.semaphore_wait(barrier, plane - 1 + ny - 1)
+    pl.semaphore_wait(barrier, guests)
     start(wave_x + wave_z + wave_y)
     get_ext.start()
     get_weights.wait()
@@ -323,18 +342,23 @@
 
     gains = [STEP * 0.5 * c for c in LAP_COEF]
 
-    def advance(buf, reach, i, below, above):
-        center = buf[reach + i, pl.ds(R, cy)]
-        near = unpack(i, below, above)
-        total = center * va[i]
-        for k in range(1, H + 1):
-            pair = buf[reach + i + k, pl.ds(R, cy)] + buf[reach + i - k, pl.ds(R, cy)]
-            pair += buf[reach + i, pl.ds(R + k, cy)] + buf[reach + i, pl.ds(R - k, cy)]
-            pair += pltpu.roll(jnp.where(at < k, near, center), cz - k, 1)
-            pair += pltpu.roll(jnp.where(at >= cz - k, near, center), k, 1)
-            total += gains[k] * pair
-        return total
-
+    band(2, [(k, gains[abs(k)]) for k in range(-H, H + 1) if k])
+
+    def advance(buf, reach, these, below, above):
+        centers = [buf[reach + i, pl.ds(R, cy)] for i in these]
+        along = along_z(centers, [unpack(i, below, above) for i in these], 2)
+        made = []
+        for at_, i in enumerate(these):
+            total = centers[at_] * va[i] + along[at_ * cy:(at_ + 1) * cy]
+            for k in range(1, H + 1):
+                pair = buf[reach + i + k, pl.ds(R, cy)] + buf[reach + i - k, pl.ds(R, cy)]
+                pair += buf[reach + i, pl.ds(R + k, cy)] + buf[reach + i, pl.ds(R - k, cy)]
+                total += gains[k] * pair
+            made.append(total)
+        return made
+
+    groups = [list(range(g, g + ZW)) for g in range(0, cx, ZW)]
+    groups = groups[:1] + groups[-1:] + groups[1:-1]
     arrive(wave_y)
     buf, reach, slot = wb, R, 0
     for s in range(SUBSTEPS):
@@ -347,39 +371,43 @@
         below, above = zin[slot, 0, 1], zin[slot, 1, 1]
         if s < SUBSTEPS - 1:
             after = psi.at[s]
-
-            def middle(i, packs, buf=buf, reach=reach, below=below, above=above, after=after):
-                value = advance(buf, reach, i, below, above)
-                after[H + i, pl.ds(R, cy)] = value
-                return pack_one(i, value, packs)
-
-            pack_out(2 + s, loop("sub", cx, middle, (zero, zero)))
-            for i in range(cx):
-                half = pl.ds(H * (i % 2), H)
-                ypack[s, 0, i // 2, half] = after[H + i, pl.ds(R, H)]
-                ypack[s, 1, i // 2, half] = after[H + i, pl.ds(R + cy - H, H)]
-            start(psi_moves[s])
+            packs = (zero, zero)
+            for n_, these in enumerate(groups):
+                for i, value in zip(these, advance(buf, reach, these, below, above)):
+                    after[H + i, pl.ds(R, cy)] = value
+                    packs = pack_one(i, value, packs)
+                    half = pl.ds(H * (i % 2), H)
+                    ypack[s, 0, i // 2, half] = value[:H]
+                    ypack[s, 1, i // 2, half] = value[cy - H:]
+                if n_ == 1:
+                    start(psi_moves[s][:2])
+            pack_out(2 + s, packs)
+            start(psi_moves[s][2:])
             buf, reach, slot = after, H, 2 + s
         else:
-            def last(i, total):
-                value = advance(buf, reach, i, below, above)
-                out_ref[i] = value
-                return total + value * value
-
-            total = loop("sub", cx, last, zero)
-
-    part = total[0:8]
-    for j in range(1, cy // 8):
-        part = part + total[8 * j:8 * j + 8]
+            total = zero
+            for these in groups:
+                for i, value in zip(these, advance(buf, reach, these, below, above)):
+                    out_ref[i] = value
+                    total = total + value * value
+
+    part = jnp.sum(total, axis=0, keepdims=True)
+    everyone = plane * ny
+    me = iy * plane + here
+
+    def any_id(d):
+        t = lax.rem(me + d, everyone)
+        p = lax.rem(t, plane)
+        return t, {"gx": lax.div(p, nz), "gy": lax.div(t, plane), "gz": lax.rem(p, nz)}
 
     def all_sum(part, slots, ssem, rsem, me, n, ids):
         if n == 1:
             return part
-        slots[n] = part
+        slots[me] = part
 
         def copy_of(d, slot):
             return pltpu.make_async_remote_copy(
-                src_ref=slots.at[n], dst_ref=slots.at[slot], send_sem=ssem.at[d], recv_sem=rsem.at[slot],
+                src_ref=slots.at[me], dst_ref=slots.at[slot], send_sem=ssem.at[d], recv_sem=rsem.at[slot],
                 device_id=ids(d)[1], device_id_type=MESH)
 
         def go(d, c):
@@ -387,21 +415,24 @@
             return c
 
         def come(d, c):
-            t = ids(d)[0]
-            copy_of(d, t).wait_recv()
-            return c + slots[t]
+            copy_of(d, ids(d)[0]).wait_recv()
+            return c
 
         def left(d, c):
             copy_of(d, me).wait_send()
             return c
 
         lax.fori_loop(1, n, go, 0)
-        total = lax.fori_loop(1, n, come, part)
+        lax.fori_loop(1, n, come, 0)
+        total = jnp.sum(slots[...], axis=0)
         lax.fori_loop(1, n, left, 0)
         return total
 
-    part = all_sum(part, sums, send2.at[0], recv2.at[0], here, plane, plane_id)
-    part = all_sum(part, sums2, send2.at[1], recv2.at[1], iy, ny, line_id)
+    if near:
+        part = all_sum(part, sums, send2.at[0], recv2.at[0], me, everyone, any_id)
+    else:
+        part = all_sum(part, sums, send2.at[0], recv2.at[0], here, plane, plane_id)
+        part = all_sum(part, sums2, send2.at[1], recv2.at[1], iy, ny, line_id)
     cells = float(cx * cy * cz * nx * ny * nz)
     scale_ref[...] = lax.rsqrt(jnp.full(scale_ref.shape, jnp.sum(part), jnp.float32) / cells + 1e-06)
     for copy, to in sent:
@@ -413,7 +444,8 @@
     nx, ny, nz = sizes
     f32 = jnp.float32
     n_messages = 36
-    most = max(nx * nz, ny)
+    summed = nx * ny * nz if nx <= 4 and ny <= 4 and nz <= 2 else nx * nz
+    most = max(summed, ny)
     vmem = pl.BlockSpec(memory_space=pltpu.VMEM)
     stay = pl.BlockSpec(memory_space=pltpu.HBM)
     psi, corr, scale = pl.pallas_call(
@@ -433,11 +465,11 @@
             pltpu.VMEM((SUBSTEPS + 1, 2, 3, cy, cz), f32),
             pltpu.VMEM((SUBSTEPS - 1, 2, cx // 2, 2 * H, cz), f32),
             pltpu.VMEM((SUBSTEPS - 1, 2, cx // 2, 2 * H, cz), f32),
-            pltpu.VMEM((2, 2 * cz, cz), f32),
+            pltpu.VMEM((3, 2 * cz, cz), f32),
             pltpu.VMEM((cx, cy, cz), f32),
             pltpu.SMEM(weights.shape, f32),
-            pltpu.VMEM((nx * nz + 1, 8, cz), f32),
-            pltpu.VMEM((ny + 1, 8, cz), f32),
+            pltpu.VMEM((summed, 1, cz), f32),
+            pltpu.VMEM((ny, 1, cz), f32),
             pltpu.SemaphoreType.DMA((n_messages,)),
             pltpu.SemaphoreType.DMA((n_messages,)),
             pltpu.SemaphoreType.DMA((2, most)),
@@ -445,8 +477,8 @@
             pltpu.SemaphoreType.DMA((3,)),
         ],
         compiler_params=pltpu.CompilerParams(collective_id=0, has_side_effects=True,
-                                             vmem_limit_bytes=67043328),
-    )(weights, wave, external)
+                                             vmem_limit_bytes=48 * 1024 * 1024),
+    )(*[pltpu.with_memory_space_constraint(x, pltpu.HBM) for x in (weights, wave, external)])
     return psi * scale[0, 0], corr
 
 

time: 48.2 us -> 41.8 us (0.87)
  Pallas kernels: 43.1 us -> 38.4 us
  other arithmetic: 2.36 us -> 1.37 us
  local copies, waits for them, and re-layouts: 1.9 us -> 1.22 us
    pallas_call x1, Pallas kernels: 43.1 us -> 38.4 us  [shards(): pl.pallas_call(functools.partial(kernel, sizes), out_shape=(jax.ShapeDtyp...]
    mul x1, other arithmetic: 2.36 us -> 1.37 us  [shards(): return (psi * scale[0, 0], corr)]
    slice x1, local copies, waits for them, and re-layouts: 1.19 us -> 0.51 us  [shards(): return (psi * scale[0, 0], corr)]
where the time goes in v4:
time: 41.8 us; the launch traced here: 41.6 us
  Pallas kernels  38.4 us (92%)
  other arithmetic  1.37 us (3%)
  local copies, waits for them, and re-layouts  1.22 us (3%)
  between operations  0.64 us (2%)
    pallas_call x1, Pallas kernels, shards(): pl.pallas_call(functools.partial(kernel, sizes), out_shape=(jax.ShapeDtyp...  38.4 us
    mul x1, other arithmetic, shards(): return (psi * scale[0, 0], corr)  1.37 us

profile of v4, /device:TPU:0, one launch (start us, length us, event | category | flops | bytes accessed | tf_op | source)
XLA Modules:
  0.0 41.6 jit_solution(14629472345255765070)
XLA Ops:
  0.6 38.4 %shard_map.50 = (f32[16,32,128]{2,1,0:T(8,128)S(1)}, f32[16,32,128]{2,1,0:T(8,128)S(1)}, f32[8,128]{1,0:T(8,128)S(1)}) custom-call(f32[3,17]{1,0:T(4,128)} %w_hbm.1, f32[16,32,128]{2,1,0:T(8,128)} %wave_hbm.1, f32[16,32,128]{2,1,0:T(8,128)} %ext_hbm.1), custom_call_target="tpu_custom_call" | custom-call | tf_op jit(solution)/shard_map/pallas_call | solution.py:451
  39.0 0.5 %slice.3 = f32[1,1]{1,0:T(1,128)} slice(f32[8,128]{1,0:T(8,128)S(1)} %get-tuple-element.6), slice={[0:1], [0:1]} | slice | bytes 8 | tf_op jit(solution)/shard_map/slice | solution.py:482
  39.6 1.4 %broadcast_multiply_fusion = f32[16,32,128]{2,1,0:T(8,128)} fusion(f32[16,32,128]{2,1,0:T(8,128)S(1)} %get-tuple-element.5, f32[]{:T(128)} %bitcast), kind=kLoop, calls=%fused_computation | loop fusion | flops 65536 | bytes 524292 | tf_op jit(solution)/shard_map/mul | solution.py:482
  40.9 0.7 %copy.6 = f32[16,32,128]{2,1,0:T(8,128)} copy(f32[16,32,128]{2,1,0:T(8,128)S(1)} %get-tuple-element.11) | data formatting | bytes 524288

commit v5 on v4

--- a/solution.py
+++ b/solution.py
@@ -69,7 +69,7 @@
 
 
 def kernel(sizes, w_hbm, wave_hbm, ext_hbm, out_ref, corr_ref, scale_ref,
-           wb, sb, xc, yb, psi, va, pack, zin, ypack, yin, bands, ext_ref, w_ref, sums, sums2,
+           wb, sb, yb, psi, va, pack, zin, ypack, yin, bands, ext_ref, w_ref, sums, sums2,
            send, recv, send2, recv2, local):
     nx, ny, nz = sizes
     cx, cy, cz = wave_hbm.shape
@@ -174,7 +174,7 @@
     def unpack(i, from_low, from_high):
         a = turn(from_high, modulo(cz - per * i, cz))
         b = turn(from_low, cz - per - per * i)
-        return jnp.where(at < per, a, b)
+        return jnp.where(lanes(a.shape) < per, a, b)
 
     def pack_out(slot, packs):
         pack[slot, 0] = packs[0]
@@ -194,10 +194,18 @@
 
     pack_out(0, loop("stage", cx, stage, (zero, zero)))
 
-    wave_x = [
-        message(wave_ref.at[pl.ds(cx - R, R)], wb.at[pl.ds(0, R), pl.ds(R, cy)], 1, 0, 0),
-        message(wave_ref.at[pl.ds(0, R)], wb.at[pl.ds(R + cx, R), pl.ds(R, cy)], -1, 0, 0),
-    ]
+    outer = [(0, R), (cy - R, R)]
+    inner = [(R, cy - 2 * R)] if cy > 2 * R else []
+
+    def x_messages(buf, y_at, bands_of_rows):
+        out = []
+        for first, rows in bands_of_rows:
+            rows = pl.ds(y_at + first, rows)
+            out.append(message(buf.at[pl.ds(cx, R), rows], buf.at[pl.ds(0, R), rows], 1, 0, 0))
+            out.append(message(buf.at[pl.ds(R, R), rows], buf.at[pl.ds(R + cx, R), rows], -1, 0, 0))
+        return out
+
+    wave_x, wave_in = x_messages(wb, R, outer), x_messages(wb, R, inner)
     wave_z = z_messages(0, True)
     wave_y = [
         message(wave_ref.at[:, pl.ds(cy - R, R)], wb.at[pl.ds(R, cx), pl.ds(0, R)], 0, 1, 0),
@@ -211,10 +219,7 @@
         ]
 
     mid_y = y_messages(yb.at[0])
-    src_x = [
-        message(sb.at[pl.ds(cx, R)], sb.at[pl.ds(0, R)], 1, 0, 0),
-        message(sb.at[pl.ds(R, R)], sb.at[pl.ds(R + cx, R)], -1, 0, 0),
-    ]
+    src_x, src_in = x_messages(sb, 0, outer), x_messages(sb, 0, inner)
     src_z = z_messages(1, True)
     end_y = y_messages(yb.at[1])
 
@@ -233,10 +238,10 @@
         psi_moves.append(moves)
 
     pl.semaphore_wait(barrier, guests)
-    start(wave_x + wave_z + wave_y)
+    start(wave_x + wave_z + wave_in + wave_y)
     get_ext.start()
     get_weights.wait()
-    for group in [wave_x, wave_z, wave_y, mid_y, src_x, src_z, end_y] + psi_moves:
+    for group in [wave_x, wave_in, wave_z, wave_y, mid_y, src_x, src_in, src_z, end_y] + psi_moves:
         blank(group)
 
     def taps_of(dim, flip):
@@ -263,40 +268,40 @@
     band(0, taps_of(2, False))
     band(1, taps_of(2, True))
 
-    def smear_xz(src, y_at, slot, square, flip, buf):
+    def smear_xz(src, y_at, slot, square, flip, buf, late, leave):
         taps = taps_of(0, flip)
-
-        def x_pass(j, c):
-            rows = pl.ds(pl.multiple_of(y_at + 8 * j, 8), 8)
-            ins = [src[k, rows] for k in range(cx + 2 * R)]
+        sides = []
+        for side in range(2):
+            near = [zin[slot, side, place] for place in range(3)]
+            if square:
+                near = [v * v for v in near]
+            sides.append(lane_taps(near[1], near[0], near[2], per, taps))
+
+        def tile(first):
+            ins = [src[k, pl.ds(y_at + first, 8)] for k in range(cx + 2 * R)]
             if square:
                 ins = [v * v for v in ins]
+            outs = []
             for i in range(cx):
                 total = None
                 for k, tap in taps:
                     part = ins[i + R + k] * tap
                     total = part if total is None else total + part
-                xc[i, pl.ds(pl.multiple_of(8 * j, 8), 8)] = total
-            return c
-
-        loop("x", cy // 8, x_pass, 0)
-        sides = []
-        for side in range(2):
-            near = [zin[slot, side, place] for place in range(3)]
-            if square:
-                near = [v * v for v in near]
-            sides.append(near)
-        below = lane_taps(sides[0][1], sides[0][0], sides[0][2], per, taps)
-        above = lane_taps(sides[1][1], sides[1][0], sides[1][2], per, taps)
-
-        def z_pass(group, c):
-            these = [group * ZW + k for k in range(ZW)]
-            made = along_z([xc[i] for i in these], [unpack(i, below, above) for i in these], int(flip))
-            for k, i in enumerate(these):
-                buf[i, pl.ds(R, cy)] = made[k * cy:(k + 1) * cy]
-            return c
-
-        loop("z", cx // ZW, z_pass, 0)
+                outs.append(total)
+            below, above = (v[first:first + 8] for v in sides)
+            made = along_z(outs, [unpack(i, below, above) for i in range(cx)], int(flip))
+            for i in range(cx):
+                buf[i, pl.ds(R + first, 8)] = made[8 * i:8 * i + 8]
+
+        for first, rows in outer:
+            for f in range(first, first + rows, 8):
+                tile(f)
+        start(leave)
+        arrive(late)
+        for first, rows in inner:
+            for f in range(first, first + rows, 8):
+                tile(f)
+        arrive(leave)
 
     def smear_y(buf, i, taps):
         total = None
@@ -306,9 +311,7 @@
         return total
 
     arrive(wave_x + wave_z)
-    smear_xz(wb, R, 0, True, False, yb.at[0])
-    start(mid_y)
-    arrive(mid_y)
+    smear_xz(wb, R, 0, True, False, yb.at[0], wave_in, mid_y)
     taps_y = taps_of(1, False)
 
     def source_pass(i, packs):
@@ -323,11 +326,9 @@
 
     pack_out(1, loop("source", cx, source_pass, (zero, zero)))
 
-    start(src_x + src_z)
+    start(src_x + src_z + src_in)
     arrive(src_x + src_z)
-    smear_xz(sb, 0, 1, False, True, yb.at[1])
-    start(end_y)
-    arrive(end_y)
+    smear_xz(sb, 0, 1, False, True, yb.at[1], src_in, end_y)
     taps_yt = taps_of(1, True)
 
     get_ext.wait()
@@ -443,7 +444,7 @@
     cx, cy, cz = wave.shape
     nx, ny, nz = sizes
     f32 = jnp.float32
-    n_messages = 36
+    n_messages = 44
     summed = nx * ny * nz if nx <= 4 and ny <= 4 and nz <= 2 else nx * nz
     most = max(summed, ny)
     vmem = pl.BlockSpec(memory_space=pltpu.VMEM)
@@ -457,7 +458,6 @@
         scratch_shapes=[
             pltpu.VMEM((cx + 2 * R, cy + 2 * R, cz), f32),
             pltpu.VMEM((cx + 2 * R, cy, cz), f32),
-            pltpu.VMEM((cx, cy, cz), f32),
             pltpu.VMEM((2, cx, cy + 2 * R, cz), f32),
             pltpu.VMEM((SUBSTEPS - 1, cx + 2 * H, cy + 2 * R, cz), f32),
             pltpu.VMEM((cx, cy, cz), f32),

time: 41.8 us -> 39.5 us (0.945)
  Pallas kernels: 38.4 us -> 36.2 us
    pallas_call x1, Pallas kernels: 38.4 us -> 36.2 us  [shards(): pl.pallas_call(functools.partial(kernel, sizes), out_shape=(jax.ShapeDtyp...]
where the time goes in v5:
time: 39.5 us; the launch traced here: 39.4 us
  Pallas kernels  36.2 us (92%)
  other arithmetic  1.37 us (3%)
  local copies, waits for them, and re-layouts  1.22 us (3%)
  between operations  0.64 us (2%)
    pallas_call x1, Pallas kernels, shards(): pl.pallas_call(functools.partial(kernel, sizes), out_shape=(jax.ShapeDtyp...  36.2 us
    mul x1, other arithmetic, shards(): return (psi * scale[0, 0], corr)  1.37 us

profile of v5, /device:TPU:0, one launch (start us, length us, event | category | flops | bytes accessed | tf_op | source)
XLA Modules:
  0.0 39.4 jit_solution(7308361573593255174)
XLA Ops:
  0.6 36.2 %shard_map.50 = (f32[16,32,128]{2,1,0:T(8,128)S(1)}, f32[16,32,128]{2,1,0:T(8,128)S(1)}, f32[8,128]{1,0:T(8,128)S(1)}) custom-call(f32[3,17]{1,0:T(4,128)} %w_hbm.1, f32[16,32,128]{2,1,0:T(8,128)} %wave_hbm.1, f32[16,32,128]{2,1,0:T(8,128)} %ext_hbm.1), custom_call_target="tpu_custom_call" | custom-call | tf_op jit(solution)/shard_map/pallas_call | solution.py:452
  36.8 0.5 %slice.3 = f32[1,1]{1,0:T(1,128)} slice(f32[8,128]{1,0:T(8,128)S(1)} %get-tuple-element.6), slice={[0:1], [0:1]} | slice | bytes 8 | tf_op jit(solution)/shard_map/slice | solution.py:482
  37.3 1.4 %broadcast_multiply_fusion = f32[16,32,128]{2,1,0:T(8,128)} fusion(f32[16,32,128]{2,1,0:T(8,128)S(1)} %get-tuple-element.5, f32[]{:T(128)} %bitcast), kind=kLoop, calls=%fused_computation | loop fusion | flops 65536 | bytes 524292 | tf_op jit(solution)/shard_map/mul | solution.py:482
  38.7 0.7 %copy.6 = f32[16,32,128]{2,1,0:T(8,128)} copy(f32[16,32,128]{2,1,0:T(8,128)S(1)} %get-tuple-element.11) | data formatting | bytes 524288

commit v6 on v5

--- a/solution.py
+++ b/solution.py
@@ -39,7 +39,7 @@
 
 
 PARTNERS = [(dx, 0, dz) for dx in (-1, 0, 1) for dz in (-1, 0, 1) if dx or dz] + [(0, 1, 0), (0, -1, 0)]
-UNROLL = {"stage": 16, "z": 2, "source": 4, "corr": 4, "sub": 4, "x": 1}
+UNROLL = {"stage": 16, "source": 16, "corr": 16}
 ZW = 4
 
 
@@ -267,6 +267,8 @@
 
     band(0, taps_of(2, False))
     band(1, taps_of(2, True))
+    gains = [STEP * 0.5 * c for c in LAP_COEF]
+    band(2, [(k, gains[abs(k)]) for k in range(-H, H + 1) if k])
 
     def smear_xz(src, y_at, slot, square, flip, buf, late, leave):
         taps = taps_of(0, flip)
@@ -341,9 +343,6 @@
 
     loop("corr", cx, corr_pass, 0)
 
-    gains = [STEP * 0.5 * c for c in LAP_COEF]
-
-    band(2, [(k, gains[abs(k)]) for k in range(-H, H + 1) if k])
 
     def advance(buf, reach, these, below, above):
         centers = [buf[reach + i, pl.ds(R, cy)] for i in these]

time: 39.5 us -> 39.2 us (level)
  Pallas kernels: 36.2 us -> 35.8 us
where the time goes in v6:
time: 39.2 us; the launch traced here: 39 us
  Pallas kernels  35.8 us (91%)
  other arithmetic  1.37 us (3%)
  local copies, waits for them, and re-layouts  1.22 us (3%)
  between operations  0.64 us (2%)
    pallas_call x1, Pallas kernels, shards(): pl.pallas_call(functools.partial(kernel, sizes), out_shape=(jax.ShapeDtyp...  35.8 us
    mul x1, other arithmetic, shards(): return (psi * scale[0, 0], corr)  1.37 us

profile of v6, /device:TPU:0, one launch (start us, length us, event | category | flops | bytes accessed | tf_op | source)
XLA Modules:
  0.0 39.0 jit_solution(14778226775452915644)
XLA Ops:
  0.6 35.8 %shard_map.50 = (f32[16,32,128]{2,1,0:T(8,128)S(1)}, f32[16,32,128]{2,1,0:T(8,128)S(1)}, f32[8,128]{1,0:T(8,128)S(1)}) custom-call(f32[3,17]{1,0:T(4,128)} %w_hbm.1, f32[16,32,128]{2,1,0:T(8,128)} %wave_hbm.1, f32[16,32,128]{2,1,0:T(8,128)} %ext_hbm.1), custom_call_target="tpu_custom_call" | custom-call | tf_op jit(solution)/shard_map/pallas_call | solution.py:451
  36.5 0.5 %slice.3 = f32[1,1]{1,0:T(1,128)} slice(f32[8,128]{1,0:T(8,128)S(1)} %get-tuple-element.6), slice={[0:1], [0:1]} | slice | bytes 8 | tf_op jit(solution)/shard_map/slice | solution.py:481
  37.0 1.4 %broadcast_multiply_fusion = f32[16,32,128]{2,1,0:T(8,128)} fusion(f32[16,32,128]{2,1,0:T(8,128)S(1)} %get-tuple-element.5, f32[]{:T(128)} %bitcast), kind=kLoop, calls=%fused_computation | loop fusion | flops 65536 | bytes 524292 | tf_op jit(solution)/shard_map/mul | solution.py:481
  38.3 0.7 %copy.6 = f32[16,32,128]{2,1,0:T(8,128)} copy(f32[16,32,128]{2,1,0:T(8,128)S(1)} %get-tuple-element.11) | data formatting | bytes 524288
